TPU v7x, 256 devices: a whole 4x4x8 slice. The times are simulated.
256 devices in a mesh: section: 4 (over y_lo, core), dp: 8 (over z), mp: 8 (over y_hi, x).
Axes of the slice: x: 4, y: 4 (y_hi: 2, y_lo: 2; y = y_hi * 2 + y_lo), z: 8, core: 2. Of those that a mesh axis runs over, the one named last changes fastest.
Arguments:
- encoder_rows: bfloat16 [96, 256, 4096], P(('section', 'dp')), may hold values from -6 to 6
- w_key: bfloat16 [4096, 4096], P(('section', 'dp'), 'mp'), may hold values from -0.09375 to 0.09375
- w_value: bfloat16 [4096, 4096], P(('section', 'dp'), 'mp'), may hold values from -0.09375 to 0.09375
- query: bfloat16 [128, 128, 4096], P(('section', 'dp'), None, 'mp'), may hold values from -80 to 80
- grad_context: bfloat16 [128, 128, 4096], P(('section', 'dp'), None, 'mp'), may hold values from -6 to 6
- source: int32 [128], replicated, may hold values from 0 to 95, as said below
Outputs:
- context: bfloat16 [128, 128, 4096], P(('section', 'dp'), None, 'mp')
- grad_query: bfloat16 [128, 128, 4096], P(('section', 'dp'), None, 'mp')
- grad_kv_weights: float32 [2, 4096, 4096], P(None, ('section', 'dp'), 'mp')
Inputs may be any that keep to these rules, and one draw needn't show every extreme that they name: `source`: the sequences of one section index (the 32 consecutive sequences held at that section index) read only examples held at the same section index; the 4 sequences of one device read examples held at 4 different dp indices.
All inputs are finite; a program needn't handle non-finite values.
Results may differ from a plain program's by a relative error of at most 0.025.
The roundings to bfloat16 on the way count: a program that leaves them out, or rounds other values in their place, can miss the bound.
Values may be sent and summed in bfloat16 or wider, within the bound.
A program may use at most 128 MiB of HBM per device.

v0:
```python
import jax
import jax.numpy as jnp
from jax import lax
from jax.sharding import PartitionSpec as P

HEAD_DIM = 64


def per_device(encoder_rows, w_key, w_value, query, grad_context, source):
    ex_dev, seq_len, width = encoder_rows.shape
    dec_dev, q_rows, inner_dev = query.shape
    heads_dev = inner_dev // HEAD_DIM
    n_dp = lax.axis_size("dp")
    section_idx = lax.axis_index("section")
    dp_idx = lax.axis_index("dp")
    flat = encoder_rows.reshape(ex_dev * seq_len, width)
    key_acc = jnp.dot(
        flat,
        lax.all_gather(w_key, ("section", "dp"), axis=0, tiled=True),
        preferred_element_type=jnp.float32,
    )
    value_acc = jnp.dot(
        flat,
        lax.all_gather(w_value, ("section", "dp"), axis=0, tiled=True),
        preferred_element_type=jnp.float32,
    )
    keys = key_acc.astype(jnp.bfloat16).reshape(ex_dev, seq_len, inner_dev)
    values = value_acc.astype(jnp.bfloat16).reshape(ex_dev, seq_len, inner_dev)
    per_section = n_dp * dec_dev
    row_plan = lax.dynamic_slice_in_dim(source, section_idx * per_section, per_section).reshape(
        n_dp, dec_dev
    )
    holder_dp = row_plan // ex_dev - section_idx * n_dp
    local_ex = row_plan % ex_dev
    mine = holder_dp == dp_idx
    wanted = mine[:, :, None] & (
        local_ex[:, :, None] == jnp.arange(ex_dev, dtype=jnp.int32)[None, None, :]
    )
    pick = jnp.sum(wanted.astype(jnp.float32), axis=1).astype(jnp.bfloat16)
    my_holder = lax.dynamic_index_in_dim(holder_dp, dp_idx, 0, keepdims=False)
    send_keys = jnp.einsum("pk,ksc->psc", pick, keys, preferred_element_type=jnp.float32).astype(
        jnp.bfloat16
    )
    send_values = jnp.einsum(
        "pk,ksc->psc", pick, values, preferred_element_type=jnp.float32
    ).astype(jnp.bfloat16)
    recv_keys, recv_values = (
        lax.all_to_all(send_keys, "dp", split_axis=0, concat_axis=0, tiled=True),
        lax.all_to_all(send_values, "dp", split_axis=0, concat_axis=0, tiled=True),
    )
    tile_keys = jnp.take(recv_keys, my_holder, axis=0)
    tile_values = jnp.take(recv_values, my_holder, axis=0)
    q_four = query.reshape(dec_dev, q_rows, heads_dev, HEAD_DIM)
    g_four = grad_context.reshape(dec_dev, q_rows, heads_dev, HEAD_DIM)
    k_four = tile_keys.reshape(dec_dev, seq_len, heads_dev, HEAD_DIM)
    v_four = tile_values.reshape(dec_dev, seq_len, heads_dev, HEAD_DIM)
    scores = jnp.einsum("nthc,nuhc->nhtu", q_four, k_four, preferred_element_type=jnp.float32)
    top = jnp.max(scores, axis=-1, keepdims=True)
    expo = jnp.exp(scores - top)
    weights = expo / jnp.sum(expo, axis=-1, keepdims=True)
    probs = weights.astype(jnp.bfloat16)
    context = jnp.einsum(
        "nhtu,nuhc->nthc", probs, v_four, preferred_element_type=jnp.float32
    ).astype(jnp.bfloat16)
    dprobs = jnp.einsum("nthc,nuhc->nhtu", g_four, v_four, preferred_element_type=jnp.float32)
    delta = jnp.sum(weights * dprobs, axis=-1, keepdims=True)
    score_grads = (weights * (dprobs - delta)).astype(jnp.bfloat16)
    grad_query = jnp.einsum(
        "nhtu,nuhc->nthc", score_grads, k_four, preferred_element_type=jnp.float32
    ).astype(jnp.bfloat16)
    key_terms = jnp.einsum(
        "nhtu,nthc->nuhc", score_grads, q_four, preferred_element_type=jnp.float32
    ).astype(jnp.bfloat16)
    value_terms = jnp.einsum(
        "nhtu,nthc->nuhc", probs, g_four, preferred_element_type=jnp.float32
    ).astype(jnp.bfloat16)
    key_terms = key_terms.reshape(dec_dev, seq_len, inner_dev)
    value_terms = value_terms.reshape(dec_dev, seq_len, inner_dev)
    to_holder = (my_holder[:, None] == jnp.arange(n_dp, dtype=jnp.int32)[None, :]).astype(
        jnp.bfloat16
    )
    back_keys = jnp.einsum(
        "np,nsc->psc", to_holder, key_terms, preferred_element_type=jnp.float32
    ).astype(jnp.bfloat16)
    back_values = jnp.einsum(
        "np,nsc->psc", to_holder, value_terms, preferred_element_type=jnp.float32
    ).astype(jnp.bfloat16)
    ret_keys, ret_values = (
        lax.all_to_all(back_keys, "dp", split_axis=0, concat_axis=0, tiled=True),
        lax.all_to_all(back_values, "dp", split_axis=0, concat_axis=0, tiled=True),
    )
    summed_keys = jnp.einsum("pk,psc->ksc", pick, ret_keys, preferred_element_type=jnp.float32)
    summed_values = jnp.einsum("pk,psc->ksc", pick, ret_values, preferred_element_type=jnp.float32)
    grad_keys = summed_keys.astype(jnp.bfloat16).reshape(ex_dev * seq_len, inner_dev)
    grad_values = summed_values.astype(jnp.bfloat16).reshape(ex_dev * seq_len, inner_dev)
    part_keys = lax.dot_general(
        flat, grad_keys, (((0,), (0,)), ((), ())), preferred_element_type=jnp.float32
    )
    part_values = lax.dot_general(
        flat, grad_values, (((0,), (0,)), ((), ())), preferred_element_type=jnp.float32
    )
    grad_rows = lax.psum_scatter(
        jnp.concatenate([part_keys, part_values], axis=1).astype(jnp.bfloat16),
        ("section", "dp"),
        scatter_dimension=0,
        tiled=True,
    ).astype(jnp.float32)
    grad_kv_weights = jnp.stack([grad_rows[:, :inner_dev], grad_rows[:, inner_dev:]], axis=0)
    return (
        context.reshape(dec_dev, q_rows, inner_dev),
        grad_query.reshape(dec_dev, q_rows, inner_dev),
        grad_kv_weights,
    )


def solution(mesh):
    return jax.shard_map(
        per_device,
        mesh=mesh,
        in_specs=(
            P(("section", "dp"), None, None),
            P(("section", "dp"), "mp"),
            P(("section", "dp"), "mp"),
            P(("section", "dp"), None, "mp"),
            P(("section", "dp"), None, "mp"),
            P(),
        ),
        out_specs=(
            P(("section", "dp"), None, "mp"),
            P(("section", "dp"), None, "mp"),
            P(None, ("section", "dp"), "mp"),
        ),
        check_vma=False,
    )
```

profile of v0, /device:TPU:1, one launch (start us, length us, event | category | flops | bytes accessed | tf_op | source)
XLA Modules:
  0.0 623.1 jit_solution(6543163994647986004)
XLA Ops:
  7.2 0.0 all-gather.3.cloned.1.call-start
  7.2 0.7 all-gather.3.cloned.1.call-update
  7.9 0.0 all-gather.5.cloned.1.call-start
  7.9 0.7 all-gather.5.cloned.1.call-update
  8.7 0.7 sign_compare_fusion
  9.4 0.1 ne.42
  9.5 0.7 broadcast_divide_fusion.1
  10.2 0.1 div.22
  10.3 0.1 rem.26
  10.4 0.1 copy.84
  10.5 0.1 copy.83
  10.6 102.7 %all-gather.3.cloned.1.call-done = bf16[4096,512]{1,0:T(8,128)(2,1)} async-done(((bf16[128,512]{1,0:T(8,128)(2,1)}), bf16[4096,512]{1,0:T(8,128)(2,1)}) %all-gather.3.cloned.1.call-update) | async-done | bytes 4194320 | tf_op jit(solution)/shard_map/all_gather | solution.py:24
  113.3 7.4 %convolution_convert_fusion.7 = bf16[768,512]{1,0:T(8,128)(2,1)S(1)} fusion(bf16[768,4096]{1,0:T(8,128)(2,1)} %bitcast.106, bf16[4096,512]{1,0:T(8,128)(2,1)} %all-gather.3.cloned.1.call-done), kind=kOutput, calls=%fused_computation.31 | convolution fusion | flops 3221618688 | bytes 11272192 | tf_op jit(solution)/shard_map/dot_general | solution.py:22
  120.8 1.1 convolution_convert_fusion.3
  121.8 2.0 copy.86
  123.9 10.4 %all-to-all-start = ((bf16[8,256,512]{2,1,0:T(8,128)(2,1)}), bf16[8,256,512]{2,1,0:T(8,128)(2,1)S(1)}, u32[]{:S(2)}, u32[]{:S(2)}) async-start(bf16[8,256,512]{2,1,0:T(8,128)(2,1)} %copy.86), calls=%async_computation | async-start | bytes 4194304 | tf_op jit(solution)/shard_map/all_to_all | solution.py:49
  134.2 108.1 %all-gather.5.cloned.1.call-done = bf16[4096,512]{1,0:T(8,128)(2,1)} async-done(((bf16[128,512]{1,0:T(8,128)(2,1)}), bf16[4096,512]{1,0:T(8,128)(2,1)}) %all-gather.5.cloned.1.call-update) | async-done | bytes 4194320 | tf_op jit(solution)/shard_map/all_gather | solution.py:19
  242.3 7.4 %convolution_convert_fusion.6 = bf16[768,512]{1,0:T(8,128)(2,1)S(1)} fusion(bf16[768,4096]{1,0:T(8,128)(2,1)} %bitcast.107, bf16[4096,512]{1,0:T(8,128)(2,1)} %all-gather.5.cloned.1.call-done), kind=kOutput, calls=%fused_computation.30 | convolution fusion | flops 3221618688 | bytes 11272192 | tf_op jit(solution)/shard_map/dot_general | solution.py:17
  249.7 1.1 convolution_convert_fusion.2
  250.8 0.0 copy-start.4
  250.8 2.0 copy.89
  252.8 0.0 all-to-all-done
  252.8 10.6 %all-to-all-start.1 = ((bf16[8,256,512]{2,1,0:T(8,128)(2,1)}), bf16[8,256,512]{2,1,0:T(8,128)(2,1)}, u32[]{:S(2)}, u32[]{:S(2)}) async-start(bf16[8,256,512]{2,1,0:T(8,128)(2,1)} %copy.89), calls=%async_computation.1 | async-start | bytes 4194304 | tf_op jit(solution)/shard_map/all_to_all | solution.py:48
  263.4 0.3 copy.91
  263.7 0.0 copy-start.1
  263.7 1.5 copy.93
  265.2 0.0 copy-start.5
  265.2 1.6 gather_fusion
  266.8 48.4 %all-to-all-done.1 = bf16[8,256,512]{2,1,0:T(8,128)(2,1)} async-done(((bf16[8,256,512]{2,1,0:T(8,128)(2,1)}), bf16[8,256,512]{2,1,0:T(8,128)(2,1)}, u32[]{:S(2)}, u32[]{:S(2)}) %all-to-all-start.1) | async-done | bytes 2097184 | tf_op jit(solution)/shard_map/all_to_all | solution.py:48
  315.3 2.2 gather_fusion.1
  317.5 2.4 broadcast_select_fusion
  319.9 1.5 copy.90
  321.4 1.3 copy.87
  322.7 3.4 fusion.40
  326.1 3.3 fusion.3
  329.4 0.1 copy-done
  329.5 1.1 fusion.5
  330.7 1.8 convolution_convert_fusion.5
  332.5 2.7 copy.96
  335.1 2.1 convolution_convert_fusion.1
  337.3 2.0 copy.97
  339.3 4.3 all-to-all-start.2
  343.6 4.1 convolution_convert_fusion.4
  347.8 2.6 copy.101
  350.4 2.1 convolution_convert_fusion
  352.6 2.0 copy.102
  354.6 37.2 %all-to-all-done.2 = bf16[8,256,512]{2,1,0:T(8,128)(2,1)} async-done(((bf16[8,256,512]{2,1,0:T(8,128)(2,1)}), bf16[8,256,512]{2,1,0:T(8,128)(2,1)}, u32[]{:S(2)}, u32[]{:S(2)}) %all-to-all-start.2) | async-done | bytes 2097184 | tf_op jit(solution)/shard_map/all_to_all | solution.py:89
  391.8 4.9 all-to-all-start.3
  396.7 0.3 reduce-scatter.4.cloned.1.call-start
  397.0 3.0 fusion.14
  400.0 8.1 %fusion.1 = bf16[4096,512]{0,1:T(8,128)(2,1)} fusion(bf16[3,256,4096]{2,1,0:T(8,128)(2,1)} %param.8, bf16[3,256,512]{2,0,1:T(4,128)(2,1)S(1)} %fusion.14), kind=kOutput, calls=%fused_computation.6 | convolution fusion | flops 3223322624 | bytes 11272192 | tf_op jit(solution)/shard_map/dot_general | solution.py:96
  408.1 38.4 %all-to-all-done.3 = bf16[8,256,512]{2,1,0:T(8,128)(2,1)} async-done(((bf16[8,256,512]{2,1,0:T(8,128)(2,1)}), bf16[8,256,512]{2,1,0:T(8,128)(2,1)}, u32[]{:S(2)}, u32[]{:S(2)}) %all-to-all-start.3) | async-done | bytes 2097184 | tf_op jit(solution)/shard_map/all_to_all | solution.py:90
  446.4 3.0 fusion.17
  449.5 8.1 %fusion.2 = bf16[4096,512]{0,1:T(8,128)(2,1)} fusion(bf16[3,256,4096]{2,1,0:T(8,128)(2,1)} %param.8, bf16[3,256,512]{2,0,1:T(4,128)(2,1)S(1)} %fusion.17), kind=kOutput, calls=%fused_computation.7 | convolution fusion | flops 3223322624 | bytes 11272192 | tf_op jit(solution)/shard_map/dot_general | solution.py:99
  457.5 7.8 %pad_maximum_fusion = bf16[4096,1024]{0,1:T(8,128)(2,1)} fusion(bf16[4096,512]{0,1:T(8,128)(2,1)} %fusion.2, bf16[4096,512]{0,1:T(8,128)(2,1)} %fusion.1), kind=kLoop, calls=%fused_computation.3 | loop fusion | flops 16777216 | bytes 16777216 | tf_op jit(solution)/shard_map/concatenate | solution.py:103
  465.4 12.0 %copy.112 = bf16[4096,1024]{1,0:T(8,128)(2,1)} copy(bf16[4096,1024]{0,1:T(8,128)(2,1)} %pad_maximum_fusion) | data formatting | bytes 16777216
  477.4 0.0 reduce-scatter.4.cloned.1.call-update
  477.4 3.8 convolution_convert_fusion.9
  481.2 2.0 copy.105
  483.2 1.3 convolution_convert_fusion.8
  484.5 2.0 copy.106
  486.5 127.8 %reduce-scatter.4.cloned.1.call-done = bf16[128,1024]{1,0:T(8,128)(2,1)} async-done(((bf16[4096,1024]{1,0:T(8,128)(2,1)}), bf16[128,1024]{1,0:T(8,128)(2,1)}) %reduce-scatter.4.cloned.1.call-update) | async-done | bytes 262160
  614.3 1.1 copy.113
  615.6 1.0 copy.107
  (17 shorter events, 0.2 us)
Async XLA Ops:
  7.2 106.2 %all-gather.3.cloned.1.call-start = ((), (), s32[]{:S(2)}) async-start(), calls=%async_computation.5 | async-start | bytes 4325376 | tf_op jit(solution)/shard_map/all_gather | solution.py:24
  7.9 234.4 %all-gather.5.cloned.1.call-start = ((), (), s32[]{:S(2)}) async-start(), calls=%async_computation.6 | async-start | bytes 4325376 | tf_op jit(solution)/shard_map/all_gather | solution.py:19
  123.9 128.9 %all-to-all-start = ((bf16[8,256,512]{2,1,0:T(8,128)(2,1)}), bf16[8,256,512]{2,1,0:T(8,128)(2,1)S(1)}, u32[]{:S(2)}, u32[]{:S(2)}) async-start(bf16[8,256,512]{2,1,0:T(8,128)(2,1)} %copy.86), calls=%async_computation | async-start | bytes 4194304 | tf_op jit(solution)/shard_map/all_to_all | solution.py:49
  250.8 12.6 %copy-start.4 = (bf16[4,128,512]{2,1,0:T(8,128)(2,1)S(1)}, bf16[4,128,512]{2,1,0:T(8,128)(2,1)}, u32[]{:S(2)}) copy-start(bf16[4,128,512]{2,1,0:T(8,128)(2,1)} %param.11) | copy-start | bytes 1572868
  252.8 62.5 %all-to-all-start.1 = ((bf16[8,256,512]{2,1,0:T(8,128)(2,1)}), bf16[8,256,512]{2,1,0:T(8,128)(2,1)}, u32[]{:S(2)}, u32[]{:S(2)}) async-start(bf16[8,256,512]{2,1,0:T(8,128)(2,1)} %copy.89), calls=%async_computation.1 | async-start | bytes 4194304 | tf_op jit(solution)/shard_map/all_to_all | solution.py:48
  263.7 59.1 %copy-start.1 = (bf16[4,128,512]{1,2,0:T(8,128)(2,1)}, bf16[4,128,512]{1,2,0:T(8,128)(2,1)S(1)}, u32[]{:S(2)}) copy-start(bf16[4,128,512]{1,2,0:T(8,128)(2,1)S(1)} %copy.91) | copy-start | bytes 1572868
  265.2 60.9 %copy-start.5 = (bf16[4,128,512]{1,2,0:T(8,128)(2,1)}, bf16[4,128,512]{1,2,0:T(8,128)(2,1)S(1)}, u32[]{:S(2)}) copy-start(bf16[4,128,512]{1,2,0:T(8,128)(2,1)S(1)} %copy.93) | copy-start | bytes 1572868
  322.7 3.4 copy-start.3
  326.1 3.5 copy-start
  329.5 1.1 copy-start.2
  339.3 52.5 %all-to-all-start.2 = ((bf16[8,256,512]{2,1,0:T(8,128)(2,1)}), bf16[8,256,512]{2,1,0:T(8,128)(2,1)}, u32[]{:S(2)}, u32[]{:S(2)}) async-start(bf16[8,256,512]{2,1,0:T(8,128)(2,1)} %copy.97), calls=%async_computation.2 | async-start | bytes 4194304 | tf_op jit(solution)/shard_map/all_to_all | solution.py:89
  391.8 54.6 %all-to-all-start.3 = ((bf16[8,256,512]{2,1,0:T(8,128)(2,1)}), bf16[8,256,512]{2,1,0:T(8,128)(2,1)}, u32[]{:S(2)}, u32[]{:S(2)}) async-start(bf16[8,256,512]{2,1,0:T(8,128)(2,1)} %copy.102), calls=%async_computation.3 | async-start | bytes 4194304 | tf_op jit(solution)/shard_map/all_to_all | solution.py:90
  396.7 217.6 %reduce-scatter.4.cloned.1.call-start = ((), (), s32[]{:S(2)}) async-start(), calls=%async_computation.7 | async-start | bytes 8650752
Sparse Core Ops, SparseCore 0:
  9.8 103.5 all-gather.2
  115.1 127.0 all-gather.4
  477.5 136.7 reduce-scatter.3
where the time goes:
time: 624 us; the launch traced here: 623 us
  waiting for transfers between devices  464 us (74%)
  matrix products  61.1 us (10%)
  local copies, waits for them, and re-layouts  40.5 us (6%)
  starting transfers between devices  30.5 us (5%)
  between operations  14 us (2%)
  other arithmetic  13 us (2%)
    unnamed x4, waiting for transfers between devices  129 us
    all_gather x1, waiting for transfers between devices, per_device(): lax.all_gather(w_key, ('section', 'dp'), axis=0, tiled=True)  108 us
    all_gather x1, waiting for transfers between devices, per_device(): lax.all_gather(w_value, ('section', 'dp'), axis=0, tiled=True)  103 us
    all_to_all x1, waiting for transfers between devices, per_device(): lax.all_to_all(send_keys, 'dp', split_axis=0, concat_axis=0, tiled=True)  48.4 us
    all_to_all x1, waiting for transfers between devices, per_device(): lax.all_to_all(back_values, 'dp', split_axis=0, concat_axis=0, tiled=True)  38.4 us
    all_to_all x1, waiting for transfers between devices, per_device(): lax.all_to_all(back_keys, 'dp', split_axis=0, concat_axis=0, tiled=True)  37.2 us
    unnamed x19, local copies, waits for them, and re-layouts  20.1 us
  transfers between devices with their start and end apart: 7, of which 6 were waited for; matrix products, arithmetic and copies ran while one was open for 9% of the time, Pallas kernels for 0%

commit v1 on v0

v1 whole, which is shorter than its diff:
```python
import functools

import jax
import jax.numpy as jnp
from jax import lax
from jax.experimental import pallas as pl
from jax.experimental.pallas import tpu as pltpu
from jax.sharding import PartitionSpec as P

HEAD_DIM = 64
MESH = pl.DeviceIdType.MESH
BF16 = jnp.bfloat16
F32 = jnp.float32
N_DP = 8
N_MP = 8
DSEQ = 4
CHUNKS = 4
CROWS = 64
SLICE = 512
WROWS = 128
WCOLS = 1024


def gather_kernel(holder_ref, w_ref, snd_ref, wf_ref, ef_ref, *scratch):
    slots, picks = scratch[0:CHUNKS], scratch[CHUNKS : 2 * CHUNKS]
    ssem, rsem, lsem = scratch[2 * CHUNKS :]
    s, d, m = lax.axis_index("section"), lax.axis_index("dp"), lax.axis_index("mp")
    sib, ypart = (s ^ 1, d, m), (s ^ 2, d, m)
    zr, zl = (s, (d + 1) % 8, m), (s, (d + 7) % 8, m)
    x, yhi = m % 4, m // 4
    xr, xl, y2 = (s, d, yhi * 4 + (x + 1) % 4), (s, d, yhi * 4 + (x + 3) % 4), (s, d, m ^ 4)

    barrier = pltpu.get_barrier_semaphore()
    peers = [sib, ypart, xr, xl, y2] + [(s, (d + k) % 8, m) for k in range(1, 8)]
    for peer in peers:
        pl.semaphore_signal(barrier, inc=1, device_id=peer, device_id_type=MESH)
    pl.semaphore_wait(barrier, len(peers))

    count = [0]
    sent = []
    local = []

    def put(src, dst, to):
        i = count[0]
        count[0] += 1
        copy = pltpu.make_async_remote_copy(
            src_ref=src, dst_ref=dst, send_sem=ssem.at[i], recv_sem=rsem.at[i],
            device_id=to, device_id_type=MESH,
        )
        copy.start()
        sent.append(copy)
        return copy

    def keep(src, dst):
        copy = pltpu.make_async_copy(src, dst, lsem.at[len(local)])
        copy.start()
        local.append(copy)
        return copy

    def wblk(sec, k):
        return wf_ref.at[sec * 8 + (d + k + 8) % 8]

    own_w = wblk(s, 0)
    w_sib = put(w_ref, own_w, sib)
    w_yp = put(w_ref, own_w, ypart)
    keep(w_ref, own_w)
    order = (4, 3, 5, 2, 6, 1, 7)
    arrive = [None] * CHUNKS
    own_slot = [None] * CHUNKS
    wz = {}
    for c in range(CHUNKS):
        rows = pl.ds(c * CROWS, CROWS)
        own_slot[c] = keep(snd_ref.at[d, rows], slots[c].at[d])
        arrive[c] = [
            put(snd_ref.at[(d + k) % 8, rows], slots[c].at[d], (s, (d + k) % 8, m)) for k in order
        ]
        if c == 1:
            wz[1] = put(w_ref, own_w, zr)
            wz[-1] = put(w_ref, own_w, zl)
    w_yp.wait_recv()
    sib_recv = [w_sib]
    sp = s ^ 2
    sib_recv.append(put(wblk(sp, 0), wblk(sp, 0), sib))
    wp = {1: put(wblk(sp, 0), wblk(sp, 0), zr), -1: put(wblk(sp, 0), wblk(sp, 0), zl)}
    yrecv = {}

    def e_blk(mm, c):
        return ef_ref.at[mm, c]

    first = [None] * CHUNKS
    second = [None] * CHUNKS
    third = [None] * CHUNKS
    row0 = yhi * 4
    m_r, m_l, m_2 = row0 + (x + 1) % 4, row0 + (x + 3) % 4, row0 + (x + 2) % 4
    half = DSEQ * CROWS // 2

    def stage1(c):
        own_slot[c].wait()
        for copy in arrive[c]:
            copy.wait_recv()
        for n in range(DSEQ):
            picks[c][pl.ds(n * CROWS, CROWS), :] = slots[c][holder_ref[n]]
        mine = e_blk(m, c)
        first[c] = (put(picks[c], mine, xr), put(picks[c], mine, xl), put(picks[c], mine, y2))
        keep(picks[c], mine)

    def stage2(c):
        to_r, to_l, to_y = first[c]
        to_r.wait_recv()
        lo = e_blk(m_l, c).at[pl.ds(0, half)]
        a = put(lo, lo, xr)
        to_l.wait_recv()
        hi = e_blk(m_r, c).at[pl.ds(half, half)]
        b = put(hi, hi, xl)
        to_y.wait_recv()
        part = e_blk(m ^ 4, c)
        second[c] = (a, b, put(part, part, xr), put(part, part, xl))

    def stage3(c):
        second[c][0].wait_recv()
        second[c][1].wait_recv()
        far = e_blk(m_2, c)
        third[c] = put(far, far, y2)

    def w_step(j):
        wz[j].wait_recv()
        right_src = wblk(s, -j)
        if j < 3:
            wz[j + 1] = put(right_src, right_src, zr)
        else:
            lo = right_src.at[pl.ds(0, WROWS // 2)]
            wz[4] = put(lo, lo, zr)
        wz[-j].wait_recv()
        left_src = wblk(s, j)
        if j < 3:
            wz[-j - 1] = put(left_src, left_src, zl)
        else:
            hi = left_src.at[pl.ds(WROWS // 2, WROWS // 2)]
            wz[-4] = put(hi, hi, zl)
        sib_recv.append(put(right_src, right_src, sib))
        sib_recv.append(put(left_src, left_src, sib))
        if j >= 2:
            yrecv[j] = put(right_src, right_src, ypart)
            yrecv[-j] = put(left_src, left_src, ypart)

    stage1(0)
    stage1(1)
    stage2(0)
    w_step(1)
    stage1(2)
    stage2(1)
    stage3(0)
    stage1(3)
    w_step(2)
    stage2(2)
    stage3(1)
    w_step(3)
    stage2(3)
    stage3(2)
    wz[4].wait_recv()
    wz[-4].wait_recv()
    far_w = wblk(s, 4)
    sib_recv.append(put(far_w, far_w, sib))
    yrecv[4] = put(far_w, far_w, ypart)
    for j in (1, -1):
        wp[j].wait_recv()
        blk = wblk(sp, -j)
        sib_recv.append(put(blk, blk, sib))
    stage3(3)
    for j in (2, -2, 3, -3, 4):
        yrecv[j].wait_recv()
        blk = wblk(sp, -j)
        sib_recv.append(put(blk, blk, sib))
    for c in range(CHUNKS):
        second[c][2].wait_recv()
        second[c][3].wait_recv()
        third[c].wait_recv()
    for copy in sib_recv:
        copy.wait_recv()
    for copy in sent:
        copy.wait_send()
    for copy in local:
        if not any(copy is other for other in own_slot):
            copy.wait()


def gather(holder, w_cat, enc_send):
    n_copies = 32 + 28 + 8 * CHUNKS
    any_spec = pl.BlockSpec(memory_space=pl.ANY)
    return pl.pallas_call(
        gather_kernel,
        out_shape=(
            jax.ShapeDtypeStruct((32, WROWS, WCOLS), BF16),
            jax.ShapeDtypeStruct((N_MP, CHUNKS, DSEQ * CROWS, SLICE), BF16),
        ),
        in_specs=[
            pl.BlockSpec(memory_space=pltpu.SMEM),
            pl.BlockSpec(memory_space=pltpu.VMEM),
            any_spec,
        ],
        out_specs=(any_spec, any_spec),
        scratch_shapes=[pltpu.VMEM((N_DP, CROWS, SLICE), BF16)] * CHUNKS
        + [pltpu.VMEM((DSEQ * CROWS, SLICE), BF16)] * CHUNKS
        + [
            pltpu.SemaphoreType.DMA((n_copies,)),
            pltpu.SemaphoreType.DMA((n_copies,)),
            pltpu.SemaphoreType.DMA((1 + 2 * CHUNKS,)),
        ],
        compiler_params=pltpu.CompilerParams(collective_id=0, has_side_effects=True),
        name="gather_rows",
    )(holder, w_cat, enc_send)


def project_kernel(e_ref, w_ref, o_ref, acc):
    i = pl.program_id(0)
    term = jnp.dot(e_ref[0], w_ref[0], preferred_element_type=F32)

    @pl.when(i == 0)
    def _():
        acc[...] = term

    @pl.when(i > 0)
    def _():
        acc[...] += term

    @pl.when(i == pl.num_programs(0) - 1)
    def _():
        o_ref[...] = acc[...].astype(BF16)


def project(enc, w):
    rows = enc.shape[1]
    return pl.pallas_call(
        project_kernel,
        grid=(N_MP,),
        out_shape=jax.ShapeDtypeStruct((rows, WCOLS), BF16),
        in_specs=[
            pl.BlockSpec((1, rows, SLICE), lambda i: (i, 0, 0)),
            pl.BlockSpec((1, SLICE, WCOLS), lambda i: (i, 0, 0)),
        ],
        out_specs=pl.BlockSpec((rows, WCOLS), lambda i: (0, 0)),
        scratch_shapes=[pltpu.VMEM((rows, WCOLS), F32)],
        name="project",
    )(enc, w)


def nt(a, b):
    return lax.dot_general(a, b, (((1,), (1,)), ((), ())), preferred_element_type=F32)


def nn(a, b):
    return lax.dot_general(a, b, (((1,), (0,)), ((), ())), preferred_element_type=F32)


def tn(a, b):
    return lax.dot_general(a, b, (((0,), (0,)), ((), ())), preferred_element_type=F32)


def attend_kernel(k_ref, v_ref, q_ref, g_ref, ctx_ref, gq_ref, kt_ref, vt_ref):
    seq = CHUNKS * CROWS
    k = k_ref[...].reshape(seq, 128)
    v = v_ref[...].reshape(seq, 128)
    q, g = q_ref[0], g_ref[0]
    rows = q.shape[0]
    low = lax.broadcasted_iota(jnp.int32, q.shape, 1) < HEAD_DIM
    zero = jnp.zeros_like(q)
    q2 = jnp.concatenate([jnp.where(low, q, zero), jnp.where(low, zero, q)], axis=0)
    g2 = jnp.concatenate([jnp.where(low, g, zero), jnp.where(low, zero, g)], axis=0)
    scores = nt(q2, k)
    top = jnp.max(scores, axis=-1, keepdims=True)
    expo = jnp.exp(scores - top)
    weights = expo / jnp.sum(expo, axis=-1, keepdims=True)
    probs = weights.astype(BF16)
    dprobs = nt(g2, v)
    delta = jnp.sum(weights * dprobs, axis=-1, keepdims=True)
    grads = (weights * (dprobs - delta)).astype(BF16)
    ctx = nn(probs, v)
    gq = nn(grads, k)
    ctx_ref[0] = jnp.where(low, ctx[:rows], ctx[rows:]).astype(BF16)
    gq_ref[0] = jnp.where(low, gq[:rows], gq[rows:]).astype(BF16)
    kt_ref[...] = tn(grads, q2).astype(BF16).reshape(kt_ref.shape)
    vt_ref[...] = tn(probs, g2).astype(BF16).reshape(vt_ref.shape)


def attend(kv, query, grad_context):
    q_rows, inner = query.shape[1:]
    pairs = inner // 128
    k_spec = pl.BlockSpec((CHUNKS, 1, CROWS, 128), lambda n, h: (0, n, 0, h))
    v_spec = pl.BlockSpec((CHUNKS, 1, CROWS, 128), lambda n, h: (0, n, 0, h + pairs))
    q_spec = pl.BlockSpec((1, q_rows, 128), lambda n, h: (n, 0, h))
    kv4 = kv.reshape(CHUNKS, DSEQ, CROWS, WCOLS)
    half = jax.ShapeDtypeStruct((CHUNKS, DSEQ, CROWS, inner), BF16)
    return pl.pallas_call(
        attend_kernel,
        grid=(DSEQ, pairs),
        out_shape=(
            jax.ShapeDtypeStruct(query.shape, BF16),
            jax.ShapeDtypeStruct(query.shape, BF16),
            half,
            half,
        ),
        in_specs=[k_spec, v_spec, q_spec, q_spec],
        out_specs=(q_spec, q_spec, k_spec, k_spec),
        name="attend",
    )(kv4, kv4, query, grad_context)


def weight_grad_kernel(e_ref, k_ref, v_ref, o_ref):
    e = e_ref[0]
    inner = k_ref.shape[1]
    o_ref[:, :inner] = tn(e, k_ref[...]).astype(BF16)
    o_ref[:, inner:] = tn(e, v_ref[...]).astype(BF16)


def weight_grad(enc, key_terms, value_terms):
    rows, inner = key_terms.shape
    return pl.pallas_call(
        weight_grad_kernel,
        grid=(N_MP,),
        out_shape=jax.ShapeDtypeStruct((N_MP * SLICE, WCOLS), BF16),
        in_specs=[
            pl.BlockSpec((1, rows, SLICE), lambda i: (i, 0, 0)),
            pl.BlockSpec((rows, inner), lambda i: (0, 0)),
            pl.BlockSpec((rows, inner), lambda i: (0, 0)),
        ],
        out_specs=pl.BlockSpec((SLICE, WCOLS), lambda i: (i, 0)),
        name="weight_grad",
    )(enc, key_terms, value_terms)


def per_device(encoder_rows, w_key, w_value, query, grad_context, source):
    ex_dev = encoder_rows.shape[0]
    dec_dev, q_rows, inner = query.shape
    s, d, m = lax.axis_index("section"), lax.axis_index("dp"), lax.axis_index("mp")
    per_section = N_DP * dec_dev
    plan = lax.dynamic_slice_in_dim(source, s * per_section, per_section).reshape(N_DP, dec_dev)
    holder_dp = plan // ex_dev - s * N_DP
    local_ex = plan % ex_dev
    chosen = jnp.sum(jnp.where(holder_dp == d, local_ex, 0), axis=1)
    my_holder = lax.dynamic_index_in_dim(holder_dp, d, 0, keepdims=False)
    columns = lax.dynamic_slice_in_dim(encoder_rows, m * SLICE, SLICE, axis=2)
    enc_send = jnp.take(columns, chosen, axis=0, mode="clip")
    w_cat = jnp.concatenate([w_key, w_value], axis=1)
    w_full, enc_full = gather(my_holder, w_cat, enc_send)
    enc = enc_full.reshape(N_MP, DSEQ * CHUNKS * CROWS, SLICE)
    kv = project(enc, w_full.reshape(N_MP, SLICE, WCOLS))
    context, grad_query, key_terms, value_terms = attend(kv, query, grad_context)
    part = weight_grad(enc, key_terms.reshape(-1, inner), value_terms.reshape(-1, inner))
    grad_rows = lax.psum_scatter(
        part, ("section", "dp"), scatter_dimension=0, tiled=True
    ).astype(F32)
    grad_kv_weights = jnp.stack([grad_rows[:, :inner], grad_rows[:, inner:]], axis=0)
    return context, grad_query, grad_kv_weights


def solution(mesh):
    return jax.shard_map(
        per_device,
        mesh=mesh,
        in_specs=(
            P(("section", "dp"), None, None),
            P(("section", "dp"), "mp"),
            P(("section", "dp"), "mp"),
            P(("section", "dp"), None, "mp"),
            P(("section", "dp"), None, "mp"),
            P(),
        ),
        out_specs=(
            P(("section", "dp"), None, "mp"),
            P(("section", "dp"), None, "mp"),
            P(None, ("section", "dp"), "mp"),
        ),
        check_vma=False,
    )
```

time: 624 us -> 328 us (0.53)
  waiting for transfers between devices: 464 us -> 135 us
  Pallas kernels: 0 us -> 169 us
  matrix products: 61.1 us -> 0 us
  local copies, waits for them, and re-layouts: 40.5 us -> 4 us
  starting transfers between devices: 30.5 us -> 0.04 us
  other arithmetic: 13 us -> 5.12 us
    all_gather x2 -> x0, waiting for transfers between devices: 211 us -> none  [the longest x1 108 us: per_device(): lax.all_gather(w_key, ('section', 'dp'), axis=0, tiled=True)]
    pallas_call x0 -> x4, Pallas kernels: none -> 169 us  [the longest x1 123 us: gather(): pl.pallas_call(gather_kernel, out_shape=(jax.ShapeDtypeStruct((32, WROWS,...]
    reduce_scatter x0 -> x1, waiting for transfers between devices: none -> 135 us  [per_device(): lax.psum_scatter(part, ('section', 'dp'), scatter_dimension=0, tiled=True)]
    unnamed x4 -> x1, waiting for transfers between devices: 129 us -> 0.02 us
    all_to_all x4 -> x0, waiting for transfers between devices: 124 us -> none  [the longest x1 48.4 us: per_device(): lax.all_to_all(send_keys, 'dp', split_axis=0, concat_axis=0, tiled=True)]
    dot_general x15 -> x0, matrix products: 57.7 us -> none  [the longest x1 8.09 us: per_device(): lax.dot_general(flat, grad_values, (((0,), (0,)), ((), ())), preferred_el...]
    all_to_all x4 -> x0, starting transfers between devices: 30.2 us -> none  [the longest x1 10.6 us: per_device(): lax.all_to_all(send_keys, 'dp', split_axis=0, concat_axis=0, tiled=True)]
    unnamed x19 -> x0, local copies, waits for them, and re-layouts: 20.1 us -> none
  transfers between devices with their start and end apart: 7 -> 1, of which waited for: 6 -> 1; matrix products, arithmetic and copies ran while one was open for 9% -> 0% of each run, Pallas kernels for 0% -> 0%
where the time goes in v1:
time: 328 us; the launch traced here: 327 us
  Pallas kernels  169 us (52%)
  waiting for transfers between devices  135 us (41%)
  between operations  14.1 us (4%)
  other arithmetic  5.12 us (2%)
  local copies, waits for them, and re-layouts  4 us (1%)
    reduce_scatter x1, waiting for transfers between devices, per_device(): lax.psum_scatter(part, ('section', 'dp'), scatter_dimension=0, tiled=True)  135 us
    pallas_call x1, Pallas kernels, gather(): pl.pallas_call(gather_kernel, out_shape=(jax.ShapeDtypeStruct((32, WROWS,...  123 us
    pallas_call x1, Pallas kernels, project(): pl.pallas_call(project_kernel, grid=(N_MP,), out_shape=jax.ShapeDtypeStru...  16.2 us
    pallas_call x1, Pallas kernels, attend(): pl.pallas_call(attend_kernel, grid=(DSEQ, pairs), out_shape=(jax.ShapeDty...  15.1 us
    pallas_call x1, Pallas kernels, weight_grad(): pl.pallas_call(weight_grad_kernel, grid=(N_MP,), out_shape=jax.ShapeDtype...  14.3 us
  transfers between devices with their start and end apart: 1, of which 1 were waited for; matrix products, arithmetic and copies ran while one was open for 0% of the time, Pallas kernels for 0%

profile of v1, /device:TPU:1, one launch (start us, length us, event | category | flops | bytes accessed | tf_op | source)
XLA Modules:
  0.0 326.8 jit_solution(6944926884461378871)
XLA Ops:
  7.2 0.0 reduce-scatter.2.cloned.1.call-start
  7.2 0.7 broadcast_divide_fusion
  8.0 0.7 sign_compare_fusion
  8.7 0.1 rem.19
  8.8 0.1 div.10
  8.8 0.1 ne.27
  8.9 0.1 fusion.2
  9.1 0.5 dynamic-slice_bitcast_fusion.holder_ref
  9.6 1.7 pad_maximum_fusion.1.w_ref
  11.3 1.2 constant_dynamic-slice_fusion
  12.5 2.0 gather_fusion
  14.5 122.9 %gather_rows.1 = (bf16[32,128,1024]{2,1,0:T(8,128)(2,1)}, bf16[8,4,256,512]{3,2,1,0:T(8,128)(2,1)}) custom-call(s32[4]{0:T(128)} %dynamic-slice_bitcast_fusion.holder_ref, bf16[128,1024]{1,0:T(8,128)(2,1)} %pad_maximum_fusion.1.w_ref, bf16[8,256,512]{2,1,0:T(8,128)(2,1)} %gather_fusion), custom_call_target="tpu_custom_call" | custom-call | tf_op jit(solution)/shard_map/gather_rows/pallas_call | solution.py:190
  137.4 16.2 %project.1 = bf16[1024,1024]{1,0:T(8,128)(2,1)} custom-call(bf16[8,1024,512]{2,1,0:T(8,128)(2,1)} %bitcast.11, bf16[8,512,1024]{2,1,0:T(8,128)(2,1)} %bitcast.15), custom_call_target="tpu_custom_call" | custom-call | tf_op jit(solution)/shard_map/project/pallas_call | solution.py:233
  153.7 15.1 %attend.1 = (bf16[4,128,512]{2,1,0:T(8,128)(2,1)}, bf16[4,128,512]{2,1,0:T(8,128)(2,1)}, bf16[4,4,64,512]{3,2,1,0:T(8,128)(2,1)}, bf16[4,4,64,512]{3,2,1,0:T(8,128)(2,1)}) custom-call(bf16[4,4,64,1024]{3,2,1,0:T(8,128)(2,1)} %bitcast.13, bf16[4,4,64,1024]{3,2,1,0:T(8,128)(2,1)} %bitcast.14, bf16[4,128,512]{2,1,0:T(8,128)(2,1)} %q_ref.1, ...), custom_call_target="tpu_custom_call" | custom-call | tf_op jit(solution)/shard_map/attend/pallas_call | solution.py:293
  168.7 14.3 %weight_grad.1 = bf16[4096,1024]{1,0:T(8,128)(2,1)} custom-call(bf16[8,1024,512]{2,1,0:T(8,128)(2,1)} %bitcast.12, bf16[1024,512]{1,0:T(8,128)(2,1)} %bitcast.16, bf16[1024,512]{1,0:T(8,128)(2,1)} %bitcast.17), custom_call_target="tpu_custom_call" | custom-call | tf_op jit(solution)/shard_map/weight_grad/pallas_call | solution.py:317
  183.0 0.0 reduce-scatter.2.cloned.1.call-update
  183.1 135.0 %reduce-scatter.2.cloned.1.call-done = bf16[128,1024]{1,0:T(8,128)(2,1)} async-done(((bf16[4096,1024]{1,0:T(8,128)(2,1)}), bf16[128,1024]{1,0:T(8,128)(2,1)}) %reduce-scatter.2.cloned.1.call-update) | async-done | bytes 262160 | tf_op jit(solution)/shard_map/reduce_scatter | solution.py:349
  318.1 1.0 convert_element_type.3
  319.2 0.8 pad_maximum_fusion
  (2 shorter events, 0.0 us)
Async XLA Ops:
  7.2 311.0 %reduce-scatter.2.cloned.1.call-start = ((), (), s32[]{:S(2)}) async-start(), calls=%async_computation.1 | async-start | bytes 8650752 | tf_op jit(solution)/shard_map/reduce_scatter | solution.py:349
Sparse Core Ops, SparseCore 0:
  183.2 134.8 reduce-scatter.1

commit v2 on v1

--- a/solution.py
+++ b/solution.py
@@ -305,25 +305,173 @@
     )(kv4, kv4, query, grad_context)
 
 
-def weight_grad_kernel(e_ref, k_ref, v_ref, o_ref):
-    e = e_ref[0]
+def reduce_kernel(e_hbm, k_ref, v_ref, o_ref, e_ref, tosib, fromsib, own, ysend, yrecv, psend, precv,
+                  zsend, zrecv, lsem, sib_s, sib_r, y_s, y_r, p_s, p_r, z_s, z_r):
+    s, d, m = lax.axis_index("section"), lax.axis_index("dp"), lax.axis_index("mp")
+    core, ylo = s % 2, s // 2
+    sib, ypart = (s ^ 1, d, m), (s ^ 2, d, m)
+    zr, zl = (s, (d + 1) % 8, m), (s, (d + 7) % 8, m)
+    loads = [pltpu.make_async_copy(e_hbm.at[i], e_ref.at[i], lsem.at[i]) for i in range(N_MP)]
+    for copy in loads:
+        copy.start()
+    barrier = pltpu.get_barrier_semaphore()
+    for peer in (sib, ypart, zr, zl):
+        pl.semaphore_signal(barrier, inc=1, device_id=peer, device_id_type=MESH)
+    pl.semaphore_wait(barrier, 4)
+    for copy in loads:
+        copy.wait()
+
+    def remote(src, dst, ss, rs, to):
+        return pltpu.make_async_remote_copy(
+            src_ref=src, dst_ref=dst, send_sem=ss, recv_sem=rs, device_id=to, device_id_type=MESH
+        )
+
+    def to_sib(i):
+        return remote(tosib.at[i], fromsib.at[i], sib_s.at[i], sib_r.at[i], sib)
+
+    def to_y(k):
+        return remote(ysend.at[k], yrecv.at[k], y_s.at[k], y_r.at[k], ypart)
+
+    def to_p(k):
+        return remote(psend.at[k], precv.at[k], p_s.at[k], p_r.at[k], zr if k == 0 else zl)
+
+    def to_z(k):
+        to = zr if k % 2 == 0 else zl
+        if k < 2:
+            rows = pl.ds(k * (WROWS // 2), WROWS // 2)
+            return remote(zsend.at[k, rows], zrecv.at[k, rows], z_s.at[k], z_r.at[k], to)
+        return remote(zsend.at[k], zrecv.at[k], z_s.at[k], z_r.at[k], to)
+
+    def columns(yy, cc, dd):
+        block = (yy * 2 + cc) * 8 + dd
+        return e_ref[block // 4, :, pl.ds(pl.multiple_of((block % 4) * WROWS, WROWS), WROWS)]
+
     inner = k_ref.shape[1]
-    o_ref[:, :inner] = tn(e, k_ref[...]).astype(BF16)
-    o_ref[:, inner:] = tn(e, v_ref[...]).astype(BF16)
+
+    def pair(cc, dd, store):
+        e = jnp.concatenate([columns(1 - ylo, cc, dd), columns(ylo, cc, dd)], axis=1)
+        store(0, tn(e, k_ref[...]))
+        store(inner, tn(e, v_ref[...]))
+
+    def absorb(k):
+        to_sib(k).wait_recv()
+        own[k] += fromsib[k].astype(F32)
+
+    def start_chain():
+        to_y(0).wait_recv()
+        total = own[0, WROWS:] + yrecv[0].astype(F32)
+        half = WROWS // 2
+        zsend[0, :half] = total[:half].astype(BF16)
+        to_z(0).start()
+        zsend[1, half:] = total[half:].astype(BF16)
+        to_z(1).start()
+
+    def step(i, carry):
+        j = (i % 2) * (4 - (i + 1) // 2) + (1 - i % 2) * (4 + i // 2)
+        dd = (d + j) % 8
+
+        def store_sib(at, value):
+            tosib[i, :, at : at + inner] = value.astype(BF16)
+
+        def store_own(at, value):
+            own[i, :, at : at + inner] = value
+
+        pair(1 - core, dd, store_sib)
+        to_sib(i).start()
+        pair(core, dd, store_own)
+
+        @pl.when(i == 6)
+        def _():
+            start_chain()
+
+        @pl.when(i > 0)
+        def _():
+            absorb(i - 1)
+
+        @pl.when((i > 0) & (i < 6))
+        def _():
+            ysend[i - 1] = own[i - 1, :WROWS].astype(BF16)
+            to_y(i - 1).start()
+
+        return carry
+
+    lax.fori_loop(0, 8, step, 0)
+    absorb(7)
+    half = WROWS // 2
+    to_y(1).wait_recv()
+    total = own[1, WROWS:] + yrecv[1].astype(F32)
+    to_z(0).wait_recv()
+    zsend[2, :half] = (total[:half] + zrecv[0, :half].astype(F32)).astype(BF16)
+    zsend[2, half:] = total[half:].astype(BF16)
+    to_z(2).start()
+    to_y(2).wait_recv()
+    total = own[2, WROWS:] + yrecv[2].astype(F32)
+    to_z(1).wait_recv()
+    zsend[3, :half] = total[:half].astype(BF16)
+    zsend[3, half:] = (total[half:] + zrecv[1, half:].astype(F32)).astype(BF16)
+    to_z(3).start()
+    for k in range(2):
+        psend[k] = own[5 + k, :WROWS].astype(BF16)
+        to_p(k).start()
+    for k in range(2):
+        to_y(3 + k).wait_recv()
+        total = own[3 + k, WROWS:] + yrecv[3 + k].astype(F32)
+        to_z(2 + k).wait_recv()
+        zsend[4 + k] = (total + zrecv[2 + k].astype(F32)).astype(BF16)
+        to_z(4 + k).start()
+    total = own[7, :WROWS]
+    for k in range(2):
+        to_p(k).wait_recv()
+        total = total + precv[k].astype(F32)
+    ysend[5] = total.astype(BF16)
+    to_y(5).start()
+    for k in range(2):
+        to_z(4 + k).wait_recv()
+        zsend[6 + k] = (own[5 + k, WROWS:] + zrecv[4 + k].astype(F32)).astype(BF16)
+        to_z(6 + k).start()
+    total = own[7, WROWS:]
+    for k in range(2):
+        to_z(6 + k).wait_recv()
+        total = total + zrecv[6 + k].astype(F32)
+    to_y(5).wait_recv()
+    total = total + yrecv[5].astype(F32)
+    o_ref[0] = total[:, :inner]
+    o_ref[1] = total[:, inner:]
+    for k in range(8):
+        to_sib(k).wait_send()
+        to_z(k).wait_send()
+    for k in range(6):
+        to_y(k).wait_send()
+    for k in range(2):
+        to_p(k).wait_send()
 
 
 def weight_grad(enc, key_terms, value_terms):
     rows, inner = key_terms.shape
+    vmem = pl.BlockSpec(memory_space=pltpu.VMEM)
+    dma = pltpu.SemaphoreType.DMA
     return pl.pallas_call(
-        weight_grad_kernel,
-        grid=(N_MP,),
-        out_shape=jax.ShapeDtypeStruct((N_MP * SLICE, WCOLS), BF16),
-        in_specs=[
-            pl.BlockSpec((1, rows, SLICE), lambda i: (i, 0, 0)),
-            pl.BlockSpec((rows, inner), lambda i: (0, 0)),
-            pl.BlockSpec((rows, inner), lambda i: (0, 0)),
+        reduce_kernel,
+        out_shape=jax.ShapeDtypeStruct((2, WROWS, inner), F32),
+        in_specs=[pl.BlockSpec(memory_space=pl.ANY), vmem, vmem],
+        out_specs=vmem,
+        scratch_shapes=[
+            pltpu.VMEM((N_MP, rows, SLICE), BF16),
+            pltpu.VMEM((8, 2 * WROWS, WCOLS), BF16),
+            pltpu.VMEM((8, 2 * WROWS, WCOLS), BF16),
+            pltpu.VMEM((8, 2 * WROWS, WCOLS), F32),
+            pltpu.VMEM((6, WROWS, WCOLS), BF16),
+            pltpu.VMEM((6, WROWS, WCOLS), BF16),
+            pltpu.VMEM((2, WROWS, WCOLS), BF16),
+            pltpu.VMEM((2, WROWS, WCOLS), BF16),
+            pltpu.VMEM((8, WROWS, WCOLS), BF16),
+            pltpu.VMEM((8, WROWS, WCOLS), BF16),
+            dma((N_MP,)), dma((8,)), dma((8,)), dma((6,)), dma((6,)),
+            dma((2,)), dma((2,)), dma((8,)), dma((8,)),
         ],
-        out_specs=pl.BlockSpec((SLICE, WCOLS), lambda i: (i, 0)),
+        compiler_params=pltpu.CompilerParams(
+            collective_id=1, has_side_effects=True, vmem_limit_bytes=56 * 2**20
+        ),
         name="weight_grad",
     )(enc, key_terms, value_terms)
 
@@ -345,11 +493,9 @@
     enc = enc_full.reshape(N_MP, DSEQ * CHUNKS * CROWS, SLICE)
     kv = project(enc, w_full.reshape(N_MP, SLICE, WCOLS))
     context, grad_query, key_terms, value_terms = attend(kv, query, grad_context)
-    part = weight_grad(enc, key_terms.reshape(-1, inner), value_terms.reshape(-1, inner))
-    grad_rows = lax.psum_scatter(
-        part, ("section", "dp"), scatter_dimension=0, tiled=True
-    ).astype(F32)
-    grad_kv_weights = jnp.stack([grad_rows[:, :inner], grad_rows[:, inner:]], axis=0)
+    grad_kv_weights = weight_grad(
+        enc, key_terms.reshape(-1, inner), value_terms.reshape(-1, inner)
+    )
     return context, grad_query, grad_kv_weights
 
 

time: 328 us -> 217 us (0.66)
  waiting for transfers between devices: 135 us -> 0 us
  Pallas kernels: 169 us -> 204 us
  between operations: 14.1 us -> 0.66 us
    reduce_scatter x1 -> x0, waiting for transfers between devices: 135 us -> none  [per_device(): lax.psum_scatter(part, ('section', 'dp'), scatter_dimension=0, tiled=True)]
    pallas_call x1, Pallas kernels: 14.3 us -> 50.3 us  [weight_grad(): pl.pallas_call(reduce_kernel, out_shape=jax.ShapeDtypeStruct((2, WROWS, i...]
  transfers between devices with their start and end apart: 1 -> 0, of which waited for: 1 -> 0; matrix products, arithmetic and copies ran while one was open for 0% -> 0% of each run, Pallas kernels for 0% -> 0%
where the time goes in v2:
time: 217 us; the launch traced here: 214 us
  Pallas kernels  204 us (94%)
  local copies, waits for them, and re-layouts  5.84 us (3%)
  other arithmetic  3.3 us (2%)
    pallas_call x1, Pallas kernels, gather(): pl.pallas_call(gather_kernel, out_shape=(jax.ShapeDtypeStruct((32, WROWS,...  123 us
    pallas_call x1, Pallas kernels, weight_grad(): pl.pallas_call(reduce_kernel, out_shape=jax.ShapeDtypeStruct((2, WROWS, i...  50.3 us
    pallas_call x1, Pallas kernels, project(): pl.pallas_call(project_kernel, grid=(N_MP,), out_shape=jax.ShapeDtypeStru...  16.2 us
    pallas_call x1, Pallas kernels, attend(): pl.pallas_call(attend_kernel, grid=(DSEQ, pairs), out_shape=(jax.ShapeDty...  15.1 us

profile of v2, /device:TPU:1, one launch (start us, length us, event | category | flops | bytes accessed | tf_op | source)
XLA Modules:
  0.0 214.3 jit_solution(14326016654308800059)
XLA Ops:
  0.6 0.7 sign_compare_fusion
  1.4 0.1 ne.27
  1.5 0.7 broadcast_divide_fusion
  2.2 0.1 div.10
  2.3 0.1 rem.19
  2.4 0.1 fusion.2
  2.5 0.5 dynamic-slice_bitcast_fusion.holder_ref
  3.0 1.7 pad_maximum_fusion.w_ref
  4.7 1.2 constant_dynamic-slice_fusion
  5.9 2.0 gather_fusion
  7.9 122.9 %gather_rows.1 = (bf16[32,128,1024]{2,1,0:T(8,128)(2,1)}, bf16[8,4,256,512]{3,2,1,0:T(8,128)(2,1)}) custom-call(s32[4]{0:T(128)} %dynamic-slice_bitcast_fusion.holder_ref, bf16[128,1024]{1,0:T(8,128)(2,1)} %pad_maximum_fusion.w_ref, bf16[8,256,512]{2,1,0:T(8,128)(2,1)} %gather_fusion), custom_call_target="tpu_custom_call" | custom-call | tf_op jit(solution)/shard_map/gather_rows/pallas_call | solution.py:190
  130.9 16.2 %project.1 = bf16[1024,1024]{1,0:T(8,128)(2,1)} custom-call(bf16[8,1024,512]{2,1,0:T(8,128)(2,1)} %bitcast.7, bf16[8,512,1024]{2,1,0:T(8,128)(2,1)} %bitcast.11), custom_call_target="tpu_custom_call" | custom-call | tf_op jit(solution)/shard_map/project/pallas_call | solution.py:233
  147.1 15.1 %attend.1 = (bf16[4,128,512]{2,1,0:T(8,128)(2,1)}, bf16[4,128,512]{2,1,0:T(8,128)(2,1)}, bf16[4,4,64,512]{3,2,1,0:T(8,128)(2,1)}, bf16[4,4,64,512]{3,2,1,0:T(8,128)(2,1)}) custom-call(bf16[4,4,64,1024]{3,2,1,0:T(8,128)(2,1)} %bitcast.9, bf16[4,4,64,1024]{3,2,1,0:T(8,128)(2,1)} %bitcast.10, bf16[4,128,512]{2,1,0:T(8,128)(2,1)} %q_ref.1, ...), custom_call_target="tpu_custom_call" | custom-call | tf_op jit(solution)/shard_map/attend/pallas_call | solution.py:293
  162.2 50.3 %weight_grad.1 = f32[2,128,512]{2,1,0:T(8,128)} custom-call(bf16[8,1024,512]{2,1,0:T(8,128)(2,1)} %bitcast.8, bf16[1024,512]{1,0:T(8,128)(2,1)} %bitcast.12, bf16[1024,512]{1,0:T(8,128)(2,1)} %bitcast.13), custom_call_target="tpu_custom_call" | custom-call | tf_op jit(solution)/shard_map/weight_grad/pallas_call | solution.py:453
  212.4 1.9 copy.10
  (1 shorter events, 0.0 us)

commit v3 on v0

v3 whole, which is shorter than its diff:
```python
import jax
import jax.numpy as jnp
from jax import lax
from jax.experimental import pallas as pl
from jax.experimental.pallas import tpu as pltpu
from jax.sharding import PartitionSpec as P

HEAD_DIM = 64
MESH = pl.DeviceIdType.MESH
BF16 = jnp.bfloat16
F32 = jnp.float32
N_DP = 8
N_MP = 8
DSEQ = 4
SEQ = 256
CHUNKS = 4
CROWS = SEQ // CHUNKS
SLICE = 512
WROWS = 128
HALF = 256
LANES = 128
GATHER_COPIES = (7 + 8) * CHUNKS + 2 * 18


def nt(a, b):
    return lax.dot_general(a, b, (((1,), (1,)), ((), ())), preferred_element_type=F32)


def nn(a, b):
    return lax.dot_general(a, b, (((1,), (0,)), ((), ())), preferred_element_type=F32)


def tn(a, b):
    return lax.dot_general(a, b, (((0,), (0,)), ((), ())), preferred_element_type=F32)


def attend_pair(k, v, q, g):
    rows = q.shape[0]
    low = lax.broadcasted_iota(jnp.int32, q.shape, 1) < HEAD_DIM
    zero = jnp.zeros_like(q)
    q2 = jnp.concatenate([jnp.where(low, q, zero), jnp.where(low, zero, q)], axis=0)
    g2 = jnp.concatenate([jnp.where(low, g, zero), jnp.where(low, zero, g)], axis=0)
    scores = nt(q2, k)
    top = jnp.max(scores, axis=-1, keepdims=True)
    expo = jnp.exp(scores - top)
    weights = expo / jnp.sum(expo, axis=-1, keepdims=True)
    probs = weights.astype(BF16)
    dprobs = nt(g2, v)
    delta = jnp.sum(weights * dprobs, axis=-1, keepdims=True)
    grads = (weights * (dprobs - delta)).astype(BF16)
    ctx = nn(probs, v)
    gq = nn(grads, k)
    return (
        jnp.where(low, ctx[:rows], ctx[rows:]).astype(BF16),
        jnp.where(low, gq[:rows], gq[rows:]).astype(BF16),
        tn(grads, q2).astype(BF16),
        tn(probs, g2).astype(BF16),
    )


def kernel(holder_ref, w_ref, q_ref, g_ref, snd_ref, ctx_ref, gq_ref, o_ref, *scratch):
    slots, picks = scratch[0:CHUNKS], scratch[CHUNKS : 2 * CHUNKS]
    (ef, wf, kv, terms, tosib, fromsib, own, ysend, yrecv, psend, precv, zsend, zrecv,
     ssem, rsem, lsem, sib_s, sib_r, y_s, y_r, p_s, p_r, z_s, z_r) = scratch[2 * CHUNKS :]
    s, d, m = lax.axis_index("section"), lax.axis_index("dp"), lax.axis_index("mp")
    core, ylo = s % 2, s // 2
    sib, ypart = (s ^ 1, d, m), (s ^ 2, d, m)
    zr, zl = (s, (d + 1) % 8, m), (s, (d + 7) % 8, m)
    x, yhi = m % 4, m // 4
    m_r, m_l, m_2 = yhi * 4 + (x + 1) % 4, yhi * 4 + (x + 3) % 4, yhi * 4 + (x + 2) % 4
    xr, xl, y2 = (s, d, m_r), (s, d, m_l), (s, d, m ^ 4)

    barrier = pltpu.get_barrier_semaphore()
    peers = [sib, ypart, xr, xl, y2] + [(s, (d + k) % 8, m) for k in range(1, 8)]
    for peer in peers:
        pl.semaphore_signal(barrier, inc=1, device_id=peer, device_id_type=MESH)

    sent, local = [], []

    def put(src, dst, to):
        i = len(sent)
        copy = pltpu.make_async_remote_copy(
            src_ref=src, dst_ref=dst, send_sem=ssem.at[i], recv_sem=rsem.at[i],
            device_id=to, device_id_type=MESH,
        )
        copy.start()
        sent.append(copy)
        return copy

    def keep(src, dst):
        copy = pltpu.make_async_copy(src, dst, lsem.at[len(local)])
        copy.start()
        local.append(copy)
        return copy

    order = (4, 3, 5, 2, 6, 1, 7)
    arrive, own_slot, own_pick = [None] * CHUNKS, [None] * CHUNKS, [None] * CHUNKS
    first, second, third = [None] * CHUNKS, [None] * CHUNKS, [None] * CHUNKS
    mid = DSEQ * CROWS // 2

    def rows_out(c):
        rows = pl.ds(c * CROWS, CROWS)
        arrive[c] = [
            put(snd_ref.at[(d + k) % 8, rows], slots[c].at[d], (s, (d + k) % 8, m)) for k in order
        ]

    def stage1(c):
        own_slot[c].wait()
        for copy in arrive[c]:
            copy.wait_recv()
        for n in range(DSEQ):
            picks[c][pl.ds(n * CROWS, CROWS), :] = slots[c][holder_ref[n]]
        mine = ef.at[m, c]
        first[c] = (put(picks[c], mine, xr), put(picks[c], mine, xl), put(picks[c], mine, y2))
        own_pick[c] = keep(picks[c], mine)

    def stage2(c):
        to_r, to_l, to_y = first[c]
        to_y.wait_recv()
        part = ef.at[m ^ 4, c]
        out_r, out_l = put(part, part, xr), put(part, part, xl)
        to_r.wait_recv()
        lo = ef.at[m_l, c, pl.ds(0, mid)]
        a = put(lo, lo, xr)
        to_l.wait_recv()
        hi = ef.at[m_r, c, pl.ds(mid, mid)]
        b = put(hi, hi, xl)
        second[c] = (a, b, out_r, out_l)

    def stage3(c):
        second[c][0].wait_recv()
        second[c][1].wait_recv()
        far = ef.at[m_2, c]
        third[c] = put(far, far, y2)

    def rows_in(c):
        second[c][2].wait_recv()
        second[c][3].wait_recv()
        third[c].wait_recv()
        own_pick[c].wait()

    w_sib, w_y, w_own = [None] * 2, [None] * 2, [None] * 2
    wz = [{}, {}]
    from_sib = [[], []]

    def wpair(h, k):
        return wf.at[h, core, (d + k + 8) % 8]

    def w_begin(h):
        mine = wf.at[h, core, d, ylo]
        w_y[h] = put(w_ref.at[h], mine, ypart)
        w_own[h] = keep(w_ref.at[h], mine)

    def w_first(h):
        w_own[h].wait()
        w_y[h].wait_recv()
        both = wpair(h, 0)
        wz[h][1] = put(both, both, zr)
        wz[h][-1] = put(both, both, zl)
        from_sib[h].append(put(both, both, sib))

    def w_step(h, j):
        wz[h][j].wait_recv()
        right = wpair(h, -j)
        if j < 3:
            wz[h][j + 1] = put(right, right, zr)
        else:
            one = right.at[ylo]
            wz[h][4] = put(one, one, zr)
        wz[h][-j].wait_recv()
        left = wpair(h, j)
        if j < 3:
            wz[h][-j - 1] = put(left, left, zl)
        else:
            one = left.at[1 - ylo]
            wz[h][-4] = put(one, one, zl)
        from_sib[h].append(put(right, right, sib))
        from_sib[h].append(put(left, left, sib))

    def w_last(h):
        wz[h][4].wait_recv()
        wz[h][-4].wait_recv()
        far = wpair(h, 4)
        from_sib[h].append(put(far, far, sib))

    def w_in(h):
        for copy in from_sib[h]:
            copy.wait_recv()

    def weight_rows(h, i):
        yy, cc, z0 = i // 4, (i // 2) % 2, (i % 2) * 4
        return [wf[h, cc, z0 + k, yy] for k in range(4)]

    def project(h, c):
        lhs = jnp.concatenate([ef[i, c] for i in range(N_MP)], axis=1)
        rhs = jnp.concatenate([r for i in range(N_MP) for r in weight_rows(h, i)], axis=0)
        out = nn(lhs, rhs).astype(BF16)
        kv[h, c] = out.reshape(DSEQ, CROWS, 2 * HALF)

    def project_range(h, lo, hi):
        def body(c, carry):
            project(h, c)
            return carry

        lax.fori_loop(lo, hi, body, 0)

    def attend_range(h, lo, hi):
        def body(t, carry):
            n, p = t // 2, t % 2
            at_k = pl.ds(pl.multiple_of(p * LANES, LANES), LANES)
            at_v = pl.ds(pl.multiple_of(p * LANES + HALF, LANES), LANES)
            at_q = pl.ds(pl.multiple_of(p * LANES + h * HALF, LANES), LANES)
            k = kv[h, :, n, :, at_k].reshape(SEQ, LANES)
            v = kv[h, :, n, :, at_v].reshape(SEQ, LANES)
            ctx, gq, kt, vt = attend_pair(k, v, q_ref[n, :, at_q], g_ref[n, :, at_q])
            ctx_ref[n, :, at_q] = ctx
            gq_ref[n, :, at_q] = gq
            terms[h, :, n, :, at_k] = kt.reshape(CHUNKS, CROWS, LANES)
            terms[h, :, n, :, at_v] = vt.reshape(CHUNKS, CROWS, LANES)
            return carry

        lax.fori_loop(lo, hi, body, 0)

    def remote(src, dst, ss, rs, to):
        return pltpu.make_async_remote_copy(
            src_ref=src, dst_ref=dst, send_sem=ss, recv_sem=rs, device_id=to, device_id_type=MESH
        )

    def to_sib(h, i):
        return remote(tosib.at[h, i], fromsib.at[h, i], sib_s.at[h, i], sib_r.at[h, i], sib)

    def to_y(h, k):
        return remote(ysend.at[h, k], yrecv.at[h, k], y_s.at[h, k], y_r.at[h, k], ypart)

    def to_p(h, k):
        to = zr if k == 0 else zl
        return remote(psend.at[h, k], precv.at[h, k], p_s.at[h, k], p_r.at[h, k], to)

    half = WROWS // 2

    def to_z(h, k):
        to = zr if k % 2 == 0 else zl
        if k < 2:
            rows = pl.ds(k * half, half)
            return remote(zsend.at[h, k, rows], zrecv.at[h, k, rows], z_s.at[h, k], z_r.at[h, k], to)
        return remote(zsend.at[h, k], zrecv.at[h, k], z_s.at[h, k], z_r.at[h, k], to)

    def columns(yy, cc, dd):
        block = (yy * 2 + cc) * 8 + dd
        at = pl.ds(pl.multiple_of((block % 4) * WROWS, WROWS), WROWS)
        return ef[block // 4, :, :, at].reshape(DSEQ * SEQ, WROWS)

    def block_pair(h, cc, dd):
        e = jnp.concatenate([columns(1 - ylo, cc, dd), columns(ylo, cc, dd)], axis=1)
        return tn(e, terms[h].reshape(DSEQ * SEQ, 2 * HALF))

    def absorb(h, k):
        to_sib(h, k).wait_recv()
        own[h, k] += fromsib[h, k].astype(F32)

    def chain4(h):
        to_y(h, 0).wait_recv()
        total = own[h, 0, WROWS:] + yrecv[h, 0].astype(F32)
        zsend[h, 0, :half] = total[:half].astype(BF16)
        to_z(h, 0).start()
        zsend[h, 1, half:] = total[half:].astype(BF16)
        to_z(h, 1).start()

    def blocks(h):
        def step(i, carry):
            j = (i % 2) * (4 - (i + 1) // 2) + (1 - i % 2) * (4 + i // 2)
            dd = (d + j) % 8
            tosib[h, i] = block_pair(h, 1 - core, dd).astype(BF16)
            to_sib(h, i).start()
            own[h, i] = block_pair(h, core, dd)

            @pl.when(i == 6)
            def _():
                chain4(h)

            @pl.when(i > 0)
            def _():
                absorb(h, i - 1)

            @pl.when((i > 0) & (i < 6))
            def _():
                ysend[h, i - 1] = own[h, i - 1, :WROWS].astype(BF16)
                to_y(h, i - 1).start()

            return carry

        lax.fori_loop(0, 8, step, 0)
        absorb(h, 7)

    def chain3(h):
        to_y(h, 1).wait_recv()
        total = own[h, 1, WROWS:] + yrecv[h, 1].astype(F32)
        to_z(h, 0).wait_recv()
        zsend[h, 2, :half] = (total[:half] + zrecv[h, 0, :half].astype(F32)).astype(BF16)
        zsend[h, 2, half:] = total[half:].astype(BF16)
        to_z(h, 2).start()
        to_y(h, 2).wait_recv()
        total = own[h, 2, WROWS:] + yrecv[h, 2].astype(F32)
        to_z(h, 1).wait_recv()
        zsend[h, 3, :half] = total[:half].astype(BF16)
        zsend[h, 3, half:] = (total[half:] + zrecv[h, 1, half:].astype(F32)).astype(BF16)
        to_z(h, 3).start()
        for k in range(2):
            psend[h, k] = own[h, 5 + k, :WROWS].astype(BF16)
            to_p(h, k).start()

    def chain2(h):
        for k in range(2):
            to_y(h, 3 + k).wait_recv()
            total = own[h, 3 + k, WROWS:] + yrecv[h, 3 + k].astype(F32)
            to_z(h, 2 + k).wait_recv()
            zsend[h, 4 + k] = (total + zrecv[h, 2 + k].astype(F32)).astype(BF16)
            to_z(h, 4 + k).start()

    def partner(h):
        total = own[h, 7, :WROWS]
        for k in range(2):
            to_p(h, k).wait_recv()
            total = total + precv[h, k].astype(F32)
        ysend[h, 5] = total.astype(BF16)
        to_y(h, 5).start()

    def chain1(h):
        for k in range(2):
            to_z(h, 4 + k).wait_recv()
            zsend[h, 6 + k] = (own[h, 5 + k, WROWS:] + zrecv[h, 4 + k].astype(F32)).astype(BF16)
            to_z(h, 6 + k).start()

    def chain0(h):
        total = own[h, 7, WROWS:]
        for k in range(2):
            to_z(h, 6 + k).wait_recv()
            total = total + zrecv[h, 6 + k].astype(F32)
        to_y(h, 5).wait_recv()
        total = total + yrecv[h, 5].astype(F32)
        at = pl.ds(h * HALF, HALF)
        o_ref[0, :, at] = total[:, :HALF]
        o_ref[1, :, at] = total[:, HALF:]

    def drain(h):
        for k in range(8):
            to_sib(h, k).wait_send()
            to_z(h, k).wait_send()
        for k in range(6):
            to_y(h, k).wait_send()
        for k in range(2):
            to_p(h, k).wait_send()

    for c in range(CHUNKS):
        own_slot[c] = keep(snd_ref.at[d, pl.ds(c * CROWS, CROWS)], slots[c].at[d])
    pl.semaphore_wait(barrier, len(peers))
    w_begin(0)
    rows_out(0)
    rows_out(1)
    w_begin(1)
    w_first(0)
    rows_out(2)
    rows_out(3)
    stage1(0)
    stage1(1)
    stage2(0)
    w_step(0, 1)
    stage1(2)
    stage2(1)
    stage3(0)
    stage1(3)
    w_step(0, 2)
    stage2(2)
    stage3(1)
    w_first(1)
    w_step(0, 3)
    stage2(3)
    stage3(2)
    w_step(1, 1)
    w_last(0)
    stage3(3)
    w_in(0)
    for c in range(CHUNKS - 1):
        rows_in(c)
    w_step(1, 2)
    project_range(0, 0, CHUNKS - 1)
    rows_in(CHUNKS - 1)
    project_range(0, CHUNKS - 1, CHUNKS)
    w_step(1, 3)
    attend_range(0, 0, 4)
    w_last(1)
    attend_range(0, 4, 8)
    blocks(0)
    w_in(1)
    project_range(1, 0, 2)
    chain3(0)
    project_range(1, 2, 4)
    chain2(0)
    attend_range(1, 0, 4)
    partner(0)
    chain1(0)
    attend_range(1, 4, 8)
    blocks(1)
    chain0(0)
    chain3(1)
    chain2(1)
    partner(1)
    chain1(1)
    chain0(1)
    for copy in sent:
        copy.wait_send()
    drain(0)
    drain(1)


def run(holder, w_halves, query, grad_context, enc_send):
    rows, inner = WROWS, query.shape[2]
    vmem = pl.BlockSpec(memory_space=pltpu.VMEM)
    dma = pltpu.SemaphoreType.DMA
    wide = 2 * HALF
    return pl.pallas_call(
        kernel,
        out_shape=(
            jax.ShapeDtypeStruct(query.shape, BF16),
            jax.ShapeDtypeStruct(query.shape, BF16),
            jax.ShapeDtypeStruct((2, rows, inner), F32),
        ),
        in_specs=[
            pl.BlockSpec(memory_space=pltpu.SMEM), vmem, vmem, vmem,
            pl.BlockSpec(memory_space=pl.ANY),
        ],
        out_specs=(vmem, vmem, vmem),
        scratch_shapes=[pltpu.VMEM((N_DP, CROWS, SLICE), BF16)] * CHUNKS
        + [pltpu.VMEM((DSEQ * CROWS, SLICE), BF16)] * CHUNKS
        + [
            pltpu.VMEM((N_MP, CHUNKS, DSEQ * CROWS, SLICE), BF16),
            pltpu.VMEM((2, 2, N_DP, 2, rows, wide), BF16),
            pltpu.VMEM((2, CHUNKS, DSEQ, CROWS, wide), BF16),
            pltpu.VMEM((2, CHUNKS, DSEQ, CROWS, wide), BF16),
            pltpu.VMEM((2, 8, 2 * rows, wide), BF16),
            pltpu.VMEM((2, 8, 2 * rows, wide), BF16),
            pltpu.VMEM((2, 8, 2 * rows, wide), F32),
            pltpu.VMEM((2, 6, rows, wide), BF16),
            pltpu.VMEM((2, 6, rows, wide), BF16),
            pltpu.VMEM((2, 2, rows, wide), BF16),
            pltpu.VMEM((2, 2, rows, wide), BF16),
            pltpu.VMEM((2, 8, rows, wide), BF16),
            pltpu.VMEM((2, 8, rows, wide), BF16),
            dma((GATHER_COPIES,)), dma((GATHER_COPIES,)), dma((2 + 2 * CHUNKS,)),
            dma((2, 8)), dma((2, 8)), dma((2, 6)), dma((2, 6)),
            dma((2, 2)), dma((2, 2)), dma((2, 8)), dma((2, 8)),
        ],
        compiler_params=pltpu.CompilerParams(
            collective_id=0, has_side_effects=True, vmem_limit_bytes=60 * 2**20
        ),
        name="cross_attention",
    )(holder, w_halves, query, grad_context, enc_send)


def per_device(encoder_rows, w_key, w_value, query, grad_context, source):
    ex_dev = encoder_rows.shape[0]
    dec_dev, q_rows, inner = query.shape
    s, d, m = lax.axis_index("section"), lax.axis_index("dp"), lax.axis_index("mp")
    per_section = N_DP * dec_dev
    plan = lax.dynamic_slice_in_dim(source, s * per_section, per_section).reshape(N_DP, dec_dev)
    holder_dp = lax.div(plan, jnp.int32(ex_dev)) - s * N_DP
    local_ex = lax.rem(plan, jnp.int32(ex_dev))
    chosen = jnp.sum(jnp.where(holder_dp == d, local_ex, 0), axis=1)
    my_holder = lax.dynamic_index_in_dim(holder_dp, d, 0, keepdims=False)
    columns = lax.dynamic_slice_in_dim(encoder_rows, m * SLICE, SLICE, axis=2)
    enc_send = jnp.take(columns, chosen, axis=0, mode="clip")
    w_halves = jnp.stack(
        [
            jnp.concatenate([w[:, h * HALF : (h + 1) * HALF] for w in (w_key, w_value)], axis=1)
            for h in range(2)
        ]
    )
    return run(my_holder, w_halves, query, grad_context, enc_send)


def solution(mesh):
    return jax.shard_map(
        per_device,
        mesh=mesh,
        in_specs=(
            P(("section", "dp"), None, None),
            P(("section", "dp"), "mp"),
            P(("section", "dp"), "mp"),
            P(("section", "dp"), None, "mp"),
            P(("section", "dp"), None, "mp"),
            P(),
        ),
        out_specs=(
            P(("section", "dp"), None, "mp"),
            P(("section", "dp"), None, "mp"),
            P(None, ("section", "dp"), "mp"),
        ),
        check_vma=False,
    )
```

time: 624 us -> 177 us (0.28)
  waiting for transfers between devices: 464 us -> 0 us
  Pallas kernels: 0 us -> 164 us
  matrix products: 61.1 us -> 0 us
  starting transfers between devices: 30.5 us -> 0 us
  local copies, waits for them, and re-layouts: 40.5 us -> 10.2 us
  between operations: 14 us -> 0.68 us
  other arithmetic: 13 us -> 1.61 us
    all_gather x2 -> x0, waiting for transfers between devices: 211 us -> none  [the longest x1 108 us: per_device(): lax.all_gather(w_key, ('section', 'dp'), axis=0, tiled=True)]
    pallas_call x0 -> x1, Pallas kernels: none -> 164 us  [run(): pl.pallas_call(kernel, out_shape=(jax.ShapeDtypeStruct(query.shape, BF16)...]
    unnamed x4 -> x0, waiting for transfers between devices: 129 us -> none
    all_to_all x4 -> x0, waiting for transfers between devices: 124 us -> none  [the longest x1 48.4 us: per_device(): lax.all_to_all(send_keys, 'dp', split_axis=0, concat_axis=0, tiled=True)]
    dot_general x15 -> x0, matrix products: 57.7 us -> none  [the longest x1 8.09 us: per_device(): lax.dot_general(flat, grad_values, (((0,), (0,)), ((), ())), preferred_el...]
    all_to_all x4 -> x0, starting transfers between devices: 30.2 us -> none  [the longest x1 10.6 us: per_device(): lax.all_to_all(send_keys, 'dp', split_axis=0, concat_axis=0, tiled=True)]
    unnamed x19 -> x5, local copies, waits for them, and re-layouts: 20.1 us -> 4.59 us
    convert_element_type x4 -> x0, local copies, waits for them, and re-layouts: 8.07 us -> none  [the longest x1 2.02 us: per_device(): send_values = jnp.einsum('pk,ksc->psc', pick, values, preferred_element_t...]
  transfers between devices with their start and end apart: 7 -> 0, of which waited for: 6 -> 0; matrix products, arithmetic and copies ran while one was open for 9% -> 0% of each run, Pallas kernels for 0% -> 0%
where the time goes in v3:
time: 177 us; the launch traced here: 176 us
  Pallas kernels  164 us (93%)
  local copies, waits for them, and re-layouts  10.2 us (6%)
    pallas_call x1, Pallas kernels, run(): pl.pallas_call(kernel, out_shape=(jax.ShapeDtypeStruct(query.shape, BF16)...  164 us
    unnamed x5, local copies, waits for them, and re-layouts  4.59 us

profile of v3, /device:TPU:1, one launch (start us, length us, event | category | flops | bytes accessed | tf_op | source)
XLA Modules:
  0.0 176.2 jit_solution(7780040005893961761)
XLA Ops:
  0.6 0.7 broadcast_remainder_fusion
  1.4 0.1 rem.7
  1.5 0.1 sub.11
  1.5 0.1 select_reduce_fusion
  1.7 0.5 dynamic-slice_bitcast_fusion.holder_ref
  2.2 0.9 fusion
  3.1 0.9 fusion.1
  4.0 0.7 pad_maximum_fusion.w_ref
  4.7 1.2 constant_dynamic-slice_fusion
  5.9 2.0 %gather_fusion = bf16[8,256,512]{2,1,0:T(8,128)(2,1)} fusion(bf16[3,256,512]{2,1,0:T(8,128)(2,1)S(1)} %constant_dynamic-slice_fusion, s32[1024]{0:T(1024)S(1)} %pad_clamp_fusion), kind=kCustom, calls=%fused_computation | custom fusion | bytes 4194336 | tf_op jit(solution)/shard_map/jit(_take)/gather | solution.py:471
  7.9 163.6 %cross_attention.1 = (bf16[4,128,512]{2,1,0:T(8,128)(2,1)}, bf16[4,128,512]{2,1,0:T(8,128)(2,1)}, f32[2,128,512]{2,1,0:T(8,128)}) custom-call(s32[4]{0:T(128)} %dynamic-slice_bitcast_fusion.holder_ref, bf16[2,128,512]{2,1,0:T(8,128)(2,1)} %pad_maximum_fusion.w_ref, bf16[4,128,512]{2,1,0:T(8,128)(2,1)} %q_ref.1, bf16[4,128,512]{2,1,0:T(8,128)(2,1)} %g_ref.1, ...), custom_call_target="tpu_custom_call" | custom-call | tf_op jit(solution)/shard_map/cross_attention/pallas_call | solution.py:421
  171.6 0.0 copy-start
  171.6 1.9 %copy.12 = bf16[4,128,512]{2,1,0:T(8,128)(2,1)} copy(bf16[4,128,512]{2,1,0:T(8,128)(2,1)} %get-tuple-element.14) | data formatting | bytes 1048576
  173.5 1.9 %copy.13 = bf16[4,128,512]{2,1,0:T(8,128)(2,1)} copy(bf16[4,128,512]{2,1,0:T(8,128)(2,1)} %get-tuple-element.15) | data formatting | bytes 1048576
  175.4 0.0 copy-done
  175.4 0.8 copy.14
  (2 shorter events, 0.0 us)
Async XLA Ops:
  171.6 3.8 %copy-start = (f32[2,128,512]{2,1,0:T(8,128)S(1)}, f32[2,128,512]{2,1,0:T(8,128)}, u32[]{:S(2)}) copy-start(f32[2,128,512]{2,1,0:T(8,128)} %get-tuple-element.16) | copy-start | bytes 1572868

commit v4 on v3

--- a/solution.py
+++ b/solution.py
@@ -13,13 +13,17 @@
 N_MP = 8
 DSEQ = 4
 SEQ = 256
-CHUNKS = 4
+CHUNKS = 8
 CROWS = SEQ // CHUNKS
 SLICE = 512
 WROWS = 128
-HALF = 256
 LANES = 128
-GATHER_COPIES = (7 + 8) * CHUNKS + 2 * 18
+EX_DEV = 3
+GROUPS = 2
+GW = SLICE // GROUPS
+PAIRS = GW // LANES
+ORDER = (4, 3, 5, 2, 6, 1, 7)
+GATHER_COPIES = 15 * CHUNKS + 17 * GROUPS
 
 
 def nt(a, b):
@@ -40,28 +44,29 @@
     zero = jnp.zeros_like(q)
     q2 = jnp.concatenate([jnp.where(low, q, zero), jnp.where(low, zero, q)], axis=0)
     g2 = jnp.concatenate([jnp.where(low, g, zero), jnp.where(low, zero, g)], axis=0)
-    scores = nt(q2, k)
-    top = jnp.max(scores, axis=-1, keepdims=True)
-    expo = jnp.exp(scores - top)
-    weights = expo / jnp.sum(expo, axis=-1, keepdims=True)
+    scores = nt(k, q2)
+    expo = jnp.exp(scores - jnp.max(scores, axis=0, keepdims=True))
+    weights = expo * (1.0 / jnp.sum(expo, axis=0, keepdims=True))
     probs = weights.astype(BF16)
-    dprobs = nt(g2, v)
-    delta = jnp.sum(weights * dprobs, axis=-1, keepdims=True)
+    dprobs = nt(v, g2)
+    delta = jnp.sum(weights * dprobs, axis=0, keepdims=True)
     grads = (weights * (dprobs - delta)).astype(BF16)
-    ctx = nn(probs, v)
-    gq = nn(grads, k)
+    ctx = tn(probs, v)
+    gq = tn(grads, k)
     return (
         jnp.where(low, ctx[:rows], ctx[rows:]).astype(BF16),
         jnp.where(low, gq[:rows], gq[rows:]).astype(BF16),
-        tn(grads, q2).astype(BF16),
-        tn(probs, g2).astype(BF16),
+        nn(grads, q2).astype(BF16),
+        nn(probs, g2).astype(BF16),
     )
 
 
-def kernel(holder_ref, w_ref, q_ref, g_ref, snd_ref, ctx_ref, gq_ref, o_ref, *scratch):
+def kernel(src_ref, e_hbm, wk_hbm, wv_hbm, q_hbm, g_hbm, ctx_ref, gq_ref, o_ref, *scratch):
     slots, picks = scratch[0:CHUNKS], scratch[CHUNKS : 2 * CHUNKS]
-    (ef, wf, kv, terms, tosib, fromsib, own, ysend, yrecv, psend, precv, zsend, zrecv,
-     ssem, rsem, lsem, sib_s, sib_r, y_s, y_r, p_s, p_r, z_s, z_r) = scratch[2 * CHUNKS :]
+    (snd, rows_ref, q_ref, g_ref, ef, wf, kv, terms, tosib, fromsib, own, ysend, yrecv, psend,
+     precv, zsend, zrecv, ssem, rsem, lsem, sib_s, sib_r, y_s, y_r, p_s, p_r, z_s, z_r) = scratch[
+        2 * CHUNKS :
+    ]
     s, d, m = lax.axis_index("section"), lax.axis_index("dp"), lax.axis_index("mp")
     core, ylo = s % 2, s // 2
     sib, ypart = (s ^ 1, d, m), (s ^ 2, d, m)
@@ -93,23 +98,39 @@
         local.append(copy)
         return copy
 
-    order = (4, 3, 5, 2, 6, 1, 7)
-    arrive, own_slot, own_pick = [None] * CHUNKS, [None] * CHUNKS, [None] * CHUNKS
+    arrive, own_pick = [None] * CHUNKS, [None] * CHUNKS
     first, second, third = [None] * CHUNKS, [None] * CHUNKS, [None] * CHUNKS
     mid = DSEQ * CROWS // 2
 
+    def source_of(reader, n):
+        at = src_ref[s * (N_DP * DSEQ) + reader * DSEQ + n]
+        return lax.div(at, jnp.int32(EX_DEV)) - s * N_DP, lax.rem(at, jnp.int32(EX_DEV))
+
+    def example_for(reader):
+        chosen = jnp.int32(0)
+        for n in range(DSEQ):
+            holder, example = source_of(reader, n)
+            chosen = chosen + jnp.where(holder == d, example, 0)
+        return chosen
+
+    def fill():
+        for k in range(N_DP):
+            chosen = example_for((d + k) % 8)
+            for c in range(CHUNKS):
+                part = rows_ref[chosen, c * CROWS : (c + 1) * CROWS, :]
+                if k:
+                    snd[k - 1, c] = part
+                else:
+                    slots[c][d] = part
+
     def rows_out(c):
-        rows = pl.ds(c * CROWS, CROWS)
-        arrive[c] = [
-            put(snd_ref.at[(d + k) % 8, rows], slots[c].at[d], (s, (d + k) % 8, m)) for k in order
-        ]
+        arrive[c] = [put(snd.at[k - 1, c], slots[c].at[d], (s, (d + k) % 8, m)) for k in ORDER]
 
     def stage1(c):
-        own_slot[c].wait()
         for copy in arrive[c]:
             copy.wait_recv()
         for n in range(DSEQ):
-            picks[c][pl.ds(n * CROWS, CROWS), :] = slots[c][holder_ref[n]]
+            picks[c][pl.ds(n * CROWS, CROWS), :] = slots[c][holders[n]]
         mine = ef.at[m, c]
         first[c] = (put(picks[c], mine, xr), put(picks[c], mine, xl), put(picks[c], mine, y2))
         own_pick[c] = keep(picks[c], mine)
@@ -139,20 +160,28 @@
         third[c].wait_recv()
         own_pick[c].wait()
 
-    w_sib, w_y, w_own = [None] * 2, [None] * 2, [None] * 2
-    wz = [{}, {}]
-    from_sib = [[], []]
+    w_y, w_own = [None] * GROUPS, [None] * GROUPS
+    wz = [{} for h in range(GROUPS)]
+    from_sib = [[] for h in range(GROUPS)]
 
     def wpair(h, k):
         return wf.at[h, core, (d + k + 8) % 8]
 
+    def w_load(h):
+        at = pl.ds(h * GW, GW)
+        mine = wf.at[h, core, d, ylo]
+        w_own[h] = (
+            keep(wk_hbm.at[:, at], mine.at[:, pl.ds(0, GW)]),
+            keep(wv_hbm.at[:, at], mine.at[:, pl.ds(GW, GW)]),
+        )
+
     def w_begin(h):
+        for copy in w_own[h]:
+            copy.wait()
         mine = wf.at[h, core, d, ylo]
-        w_y[h] = put(w_ref.at[h], mine, ypart)
-        w_own[h] = keep(w_ref.at[h], mine)
+        w_y[h] = put(mine, mine, ypart)
 
     def w_first(h):
-        w_own[h].wait()
         w_y[h].wait_recv()
         both = wpair(h, 0)
         wz[h][1] = put(both, both, zr)
@@ -195,7 +224,7 @@
         lhs = jnp.concatenate([ef[i, c] for i in range(N_MP)], axis=1)
         rhs = jnp.concatenate([r for i in range(N_MP) for r in weight_rows(h, i)], axis=0)
         out = nn(lhs, rhs).astype(BF16)
-        kv[h, c] = out.reshape(DSEQ, CROWS, 2 * HALF)
+        kv[h, c] = out.reshape(DSEQ, CROWS, 2 * GW)
 
     def project_range(h, lo, hi):
         def body(c, carry):
@@ -206,10 +235,10 @@
 
     def attend_range(h, lo, hi):
         def body(t, carry):
-            n, p = t // 2, t % 2
+            n, p = t // PAIRS, t % PAIRS
             at_k = pl.ds(pl.multiple_of(p * LANES, LANES), LANES)
-            at_v = pl.ds(pl.multiple_of(p * LANES + HALF, LANES), LANES)
-            at_q = pl.ds(pl.multiple_of(p * LANES + h * HALF, LANES), LANES)
+            at_v = pl.ds(pl.multiple_of(p * LANES + GW, LANES), LANES)
+            at_q = pl.ds(pl.multiple_of(p * LANES + h * GW, LANES), LANES)
             k = kv[h, :, n, :, at_k].reshape(SEQ, LANES)
             v = kv[h, :, n, :, at_v].reshape(SEQ, LANES)
             ctx, gq, kt, vt = attend_pair(k, v, q_ref[n, :, at_q], g_ref[n, :, at_q])
@@ -233,7 +262,7 @@
         return remote(ysend.at[h, k], yrecv.at[h, k], y_s.at[h, k], y_r.at[h, k], ypart)
 
     def to_p(h, k):
-        to = zr if k == 0 else zl
+        to = zr if k % 2 == 0 else zl
         return remote(psend.at[h, k], precv.at[h, k], p_s.at[h, k], p_r.at[h, k], to)
 
     half = WROWS // 2
@@ -252,7 +281,7 @@
 
     def block_pair(h, cc, dd):
         e = jnp.concatenate([columns(1 - ylo, cc, dd), columns(ylo, cc, dd)], axis=1)
-        return tn(e, terms[h].reshape(DSEQ * SEQ, 2 * HALF))
+        return tn(e, terms[h].reshape(DSEQ * SEQ, 2 * GW))
 
     def absorb(h, k):
         to_sib(h, k).wait_recv()
@@ -282,10 +311,17 @@
             def _():
                 absorb(h, i - 1)
 
-            @pl.when((i > 0) & (i < 6))
+            @pl.when((i > 0) & (i < 4))
             def _():
                 ysend[h, i - 1] = own[h, i - 1, :WROWS].astype(BF16)
                 to_y(h, i - 1).start()
+
+            for k in range(2):
+
+                @pl.when(i == 4 + k)
+                def _(k=k):
+                    psend[h, k] = own[h, 3 + k, :WROWS].astype(BF16)
+                    to_p(h, k).start()
 
             return carry
 
@@ -306,24 +342,23 @@
         zsend[h, 3, half:] = (total[half:] + zrecv[h, 1, half:].astype(F32)).astype(BF16)
         to_z(h, 3).start()
         for k in range(2):
-            psend[h, k] = own[h, 5 + k, :WROWS].astype(BF16)
-            to_p(h, k).start()
+            to_p(h, k).wait_recv()
+            psend[h, 2 + k] = (own[h, 5 + k, :WROWS] + precv[h, k].astype(F32)).astype(BF16)
+            to_p(h, 2 + k).start()
 
     def chain2(h):
         for k in range(2):
-            to_y(h, 3 + k).wait_recv()
-            total = own[h, 3 + k, WROWS:] + yrecv[h, 3 + k].astype(F32)
             to_z(h, 2 + k).wait_recv()
-            zsend[h, 4 + k] = (total + zrecv[h, 2 + k].astype(F32)).astype(BF16)
+            zsend[h, 4 + k] = (own[h, 3 + k, WROWS:] + zrecv[h, 2 + k].astype(F32)).astype(BF16)
             to_z(h, 4 + k).start()
 
     def partner(h):
         total = own[h, 7, :WROWS]
         for k in range(2):
-            to_p(h, k).wait_recv()
-            total = total + precv[h, k].astype(F32)
-        ysend[h, 5] = total.astype(BF16)
-        to_y(h, 5).start()
+            to_p(h, 2 + k).wait_recv()
+            total = total + precv[h, 2 + k].astype(F32)
+        ysend[h, 3] = total.astype(BF16)
+        to_y(h, 3).start()
 
     def chain1(h):
         for k in range(2):
@@ -336,65 +371,80 @@
         for k in range(2):
             to_z(h, 6 + k).wait_recv()
             total = total + zrecv[h, 6 + k].astype(F32)
-        to_y(h, 5).wait_recv()
-        total = total + yrecv[h, 5].astype(F32)
-        at = pl.ds(h * HALF, HALF)
-        o_ref[0, :, at] = total[:, :HALF]
-        o_ref[1, :, at] = total[:, HALF:]
+        to_y(h, 3).wait_recv()
+        total = total + yrecv[h, 3].astype(F32)
+        at = pl.ds(h * GW, GW)
+        o_ref[0, :, at] = total[:, :GW]
+        o_ref[1, :, at] = total[:, GW:]
 
     def drain(h):
         for k in range(8):
             to_sib(h, k).wait_send()
             to_z(h, k).wait_send()
-        for k in range(6):
+        for k in range(4):
             to_y(h, k).wait_send()
-        for k in range(2):
             to_p(h, k).wait_send()
 
-    for c in range(CHUNKS):
-        own_slot[c] = keep(snd_ref.at[d, pl.ds(c * CROWS, CROWS)], slots[c].at[d])
+    rows_copy = keep(e_hbm.at[:, :, pl.ds(m * SLICE, SLICE)], rows_ref)
+    for h in range(GROUPS):
+        w_load(h)
+    late = (keep(q_hbm, q_ref), keep(g_hbm, g_ref))
+    holders = [jnp.clip(source_of(d, n)[0], 0, N_DP - 1) for n in range(DSEQ)]
+    rows_copy.wait()
+    fill()
     pl.semaphore_wait(barrier, len(peers))
-    w_begin(0)
-    rows_out(0)
-    rows_out(1)
-    w_begin(1)
+    for h in range(GROUPS):
+        w_begin(h)
+    for c in range(6):
+        rows_out(c)
     w_first(0)
-    rows_out(2)
-    rows_out(3)
+    rows_out(6)
+    rows_out(7)
     stage1(0)
+    stage2(0)
     stage1(1)
-    stage2(0)
+    stage3(0)
+    stage2(1)
+    stage1(2)
+    stage3(1)
+    stage1(3)
+    stage2(2)
+    stage3(2)
+    stage1(4)
+    stage2(3)
+    stage1(5)
+    stage3(3)
+    stage2(4)
     w_step(0, 1)
-    stage1(2)
-    stage2(1)
-    stage3(0)
-    stage1(3)
+    stage3(4)
+    stage2(5)
+    stage1(6)
+    stage3(5)
+    stage1(7)
+    stage2(6)
+    stage3(6)
     w_step(0, 2)
-    stage2(2)
-    stage3(1)
+    stage2(7)
     w_first(1)
+    stage3(7)
     w_step(0, 3)
-    stage2(3)
-    stage3(2)
     w_step(1, 1)
     w_last(0)
-    stage3(3)
+    for c in range(CHUNKS):
+        rows_in(c)
     w_in(0)
-    for c in range(CHUNKS - 1):
-        rows_in(c)
+    project_range(0, 0, CHUNKS)
     w_step(1, 2)
-    project_range(0, 0, CHUNKS - 1)
-    rows_in(CHUNKS - 1)
-    project_range(0, CHUNKS - 1, CHUNKS)
+    for copy in late:
+        copy.wait()
+    attend_range(0, 0, 8)
     w_step(1, 3)
-    attend_range(0, 0, 4)
+    blocks(0)
     w_last(1)
-    attend_range(0, 4, 8)
-    blocks(0)
     w_in(1)
-    project_range(1, 0, 2)
+    project_range(1, 0, 4)
     chain3(0)
-    project_range(1, 2, 4)
+    project_range(1, 4, 8)
     chain2(0)
     attend_range(1, 0, 4)
     partner(0)
@@ -409,15 +459,16 @@
     chain0(1)
     for copy in sent:
         copy.wait_send()
-    drain(0)
-    drain(1)
-
-
-def run(holder, w_halves, query, grad_context, enc_send):
-    rows, inner = WROWS, query.shape[2]
+    for h in range(GROUPS):
+        drain(h)
+
+
+def per_device(encoder_rows, w_key, w_value, query, grad_context, source):
+    rows, inner = w_key.shape
     vmem = pl.BlockSpec(memory_space=pltpu.VMEM)
+    hbm = pl.BlockSpec(memory_space=pl.ANY)
     dma = pltpu.SemaphoreType.DMA
-    wide = 2 * HALF
+    wide = 2 * GW
     return pl.pallas_call(
         kernel,
         out_shape=(
@@ -425,57 +476,37 @@
             jax.ShapeDtypeStruct(query.shape, BF16),
             jax.ShapeDtypeStruct((2, rows, inner), F32),
         ),
-        in_specs=[
-            pl.BlockSpec(memory_space=pltpu.SMEM), vmem, vmem, vmem,
-            pl.BlockSpec(memory_space=pl.ANY),
-        ],
+        in_specs=[pl.BlockSpec(memory_space=pltpu.SMEM), hbm, hbm, hbm, hbm, hbm],
         out_specs=(vmem, vmem, vmem),
         scratch_shapes=[pltpu.VMEM((N_DP, CROWS, SLICE), BF16)] * CHUNKS
         + [pltpu.VMEM((DSEQ * CROWS, SLICE), BF16)] * CHUNKS
         + [
+            pltpu.VMEM((N_DP - 1, CHUNKS, CROWS, SLICE), BF16),
+            pltpu.VMEM((EX_DEV, SEQ, SLICE), BF16),
+            pltpu.VMEM(query.shape, BF16),
+            pltpu.VMEM(query.shape, BF16),
             pltpu.VMEM((N_MP, CHUNKS, DSEQ * CROWS, SLICE), BF16),
-            pltpu.VMEM((2, 2, N_DP, 2, rows, wide), BF16),
-            pltpu.VMEM((2, CHUNKS, DSEQ, CROWS, wide), BF16),
-            pltpu.VMEM((2, CHUNKS, DSEQ, CROWS, wide), BF16),
-            pltpu.VMEM((2, 8, 2 * rows, wide), BF16),
-            pltpu.VMEM((2, 8, 2 * rows, wide), BF16),
-            pltpu.VMEM((2, 8, 2 * rows, wide), F32),
-            pltpu.VMEM((2, 6, rows, wide), BF16),
-            pltpu.VMEM((2, 6, rows, wide), BF16),
-            pltpu.VMEM((2, 2, rows, wide), BF16),
-            pltpu.VMEM((2, 2, rows, wide), BF16),
-            pltpu.VMEM((2, 8, rows, wide), BF16),
-            pltpu.VMEM((2, 8, rows, wide), BF16),
-            dma((GATHER_COPIES,)), dma((GATHER_COPIES,)), dma((2 + 2 * CHUNKS,)),
-            dma((2, 8)), dma((2, 8)), dma((2, 6)), dma((2, 6)),
-            dma((2, 2)), dma((2, 2)), dma((2, 8)), dma((2, 8)),
+            pltpu.VMEM((GROUPS, 2, N_DP, 2, rows, wide), BF16),
+            pltpu.VMEM((GROUPS, CHUNKS, DSEQ, CROWS, wide), BF16),
+            pltpu.VMEM((GROUPS, CHUNKS, DSEQ, CROWS, wide), BF16),
+            pltpu.VMEM((GROUPS, 8, 2 * rows, wide), BF16),
+            pltpu.VMEM((GROUPS, 8, 2 * rows, wide), BF16),
+            pltpu.VMEM((GROUPS, 8, 2 * rows, wide), F32),
+            pltpu.VMEM((GROUPS, 4, rows, wide), BF16),
+            pltpu.VMEM((GROUPS, 4, rows, wide), BF16),
+            pltpu.VMEM((GROUPS, 4, rows, wide), BF16),
+            pltpu.VMEM((GROUPS, 4, rows, wide), BF16),
+            pltpu.VMEM((GROUPS, 8, rows, wide), BF16),
+            pltpu.VMEM((GROUPS, 8, rows, wide), BF16),
+            dma((GATHER_COPIES,)), dma((GATHER_COPIES,)), dma((3 + 2 * GROUPS + CHUNKS,)),
+            dma((GROUPS, 8)), dma((GROUPS, 8)), dma((GROUPS, 4)), dma((GROUPS, 4)),
+            dma((GROUPS, 4)), dma((GROUPS, 4)), dma((GROUPS, 8)), dma((GROUPS, 8)),
         ],
         compiler_params=pltpu.CompilerParams(
-            collective_id=0, has_side_effects=True, vmem_limit_bytes=60 * 2**20
+            collective_id=0, has_side_effects=True, vmem_limit_bytes=61 * 2**20
         ),
         name="cross_attention",
-    )(holder, w_halves, query, grad_context, enc_send)
-
-
-def per_device(encoder_rows, w_key, w_value, query, grad_context, source):
-    ex_dev = encoder_rows.shape[0]
-    dec_dev, q_rows, inner = query.shape
-    s, d, m = lax.axis_index("section"), lax.axis_index("dp"), lax.axis_index("mp")
-    per_section = N_DP * dec_dev
-    plan = lax.dynamic_slice_in_dim(source, s * per_section, per_section).reshape(N_DP, dec_dev)
-    holder_dp = lax.div(plan, jnp.int32(ex_dev)) - s * N_DP
-    local_ex = lax.rem(plan, jnp.int32(ex_dev))
-    chosen = jnp.sum(jnp.where(holder_dp == d, local_ex, 0), axis=1)
-    my_holder = lax.dynamic_index_in_dim(holder_dp, d, 0, keepdims=False)
-    columns = lax.dynamic_slice_in_dim(encoder_rows, m * SLICE, SLICE, axis=2)
-    enc_send = jnp.take(columns, chosen, axis=0, mode="clip")
-    w_halves = jnp.stack(
-        [
-            jnp.concatenate([w[:, h * HALF : (h + 1) * HALF] for w in (w_key, w_value)], axis=1)
-            for h in range(2)
-        ]
-    )
-    return run(my_holder, w_halves, query, grad_context, enc_send)
+    )(source, encoder_rows, w_key, w_value, query, grad_context)
 
 
 def solution(mesh):

time: 177 us -> 171 us (0.966)
  local copies, waits for them, and re-layouts: 10.2 us -> 5.6 us
    gather x1 -> x0, local copies, waits for them, and re-layouts: 2.01 us -> none  [per_device(): enc_send = jnp.take(columns, chosen, axis=0, mode='clip')]
    unnamed x5 -> x3, local copies, waits for them, and re-layouts: 4.59 us -> 5.6 us
where the time goes in v4:
time: 171 us
  Pallas kernels  164 us (96%)
  local copies, waits for them, and re-layouts  5.6 us (3%)
    pallas_call x1, Pallas kernels, per_device(): pl.pallas_call(kernel, out_shape=(jax.ShapeDtypeStruct(query.shape, BF16)...  164 us
    unnamed x3, local copies, waits for them, and re-layouts  5.6 us

profile of v4, /device:TPU:1, one launch (start us, length us, event | category | flops | bytes accessed | tf_op | source)
XLA Modules:
  0.0 170.5 jit_solution(13602003731883390979)
XLA Ops:
  0.6 164.3 %cross_attention.1 = (bf16[4,128,512]{2,1,0:T(8,128)(2,1)}, bf16[4,128,512]{2,1,0:T(8,128)(2,1)}, f32[2,128,512]{2,1,0:T(8,128)}) custom-call(s32[128]{0:T(128)} %src_ref.1, bf16[3,256,4096]{2,1,0:T(8,128)(2,1)} %e_hbm.1, bf16[128,512]{1,0:T(8,128)(2,1)} %wk_hbm.1, bf16[128,512]{1,0:T(8,128)(2,1)} %wv_hbm.1, bf16[4,128,512]{2,1,0:T(8,128)(2,1)} %q_hbm.1, ...), custom_call_target="tpu_custom_call" | custom-call | tf_op jit(solution)/shard_map/cross_attention/pallas_call | solution.py:472
  164.9 1.9 %copy.12 = bf16[4,128,512]{2,1,0:T(8,128)(2,1)} copy(bf16[4,128,512]{2,1,0:T(8,128)(2,1)} %get-tuple-element.6) | data formatting | bytes 1048576
  166.8 1.9 %copy.13 = bf16[4,128,512]{2,1,0:T(8,128)(2,1)} copy(bf16[4,128,512]{2,1,0:T(8,128)(2,1)} %get-tuple-element.7) | data formatting | bytes 1048576
  168.7 1.9 %copy.14 = f32[2,128,512]{2,1,0:T(8,128)} copy(f32[2,128,512]{2,1,0:T(8,128)} %get-tuple-element.8) | data formatting | bytes 1048576

commit v5 on v4

--- a/solution.py
+++ b/solution.py
@@ -23,7 +23,8 @@
 GW = SLICE // GROUPS
 PAIRS = GW // LANES
 ORDER = (4, 3, 5, 2, 6, 1, 7)
-GATHER_COPIES = 15 * CHUNKS + 17 * GROUPS
+LIGHT = (7,)
+GATHER_COPIES = 15 * CHUNKS + 2 * len(LIGHT) + 17 * GROUPS
 
 
 def nt(a, b):
@@ -149,15 +150,24 @@
         second[c] = (a, b, out_r, out_l)
 
     def stage3(c):
-        second[c][0].wait_recv()
-        second[c][1].wait_recv()
-        far = ef.at[m_2, c]
-        third[c] = put(far, far, y2)
+        if c in LIGHT:
+            a, b, out_r, out_l = second[c]
+            out_r.wait_recv()
+            lo = ef.at[m_l ^ 4, c, pl.ds(0, mid)]
+            far_a = put(lo, lo, xr)
+            out_l.wait_recv()
+            hi = ef.at[m_r ^ 4, c, pl.ds(mid, mid)]
+            far_b = put(hi, hi, xl)
+            third[c] = (a, b, far_a, far_b)
+        else:
+            second[c][0].wait_recv()
+            second[c][1].wait_recv()
+            far = ef.at[m_2, c]
+            third[c] = (second[c][2], second[c][3], put(far, far, y2))
 
     def rows_in(c):
-        second[c][2].wait_recv()
-        second[c][3].wait_recv()
-        third[c].wait_recv()
+        for copy in third[c]:
+            copy.wait_recv()
         own_pick[c].wait()
 
     w_y, w_own = [None] * GROUPS, [None] * GROUPS
@@ -220,18 +230,11 @@
         yy, cc, z0 = i // 4, (i // 2) % 2, (i % 2) * 4
         return [wf[h, cc, z0 + k, yy] for k in range(4)]
 
-    def project(h, c):
-        lhs = jnp.concatenate([ef[i, c] for i in range(N_MP)], axis=1)
+    def project_range(h, lo, hi):
+        rows = (hi - lo) * DSEQ * CROWS
+        lhs = jnp.concatenate([ef[i, lo:hi].reshape(rows, SLICE) for i in range(N_MP)], axis=1)
         rhs = jnp.concatenate([r for i in range(N_MP) for r in weight_rows(h, i)], axis=0)
-        out = nn(lhs, rhs).astype(BF16)
-        kv[h, c] = out.reshape(DSEQ, CROWS, 2 * GW)
-
-    def project_range(h, lo, hi):
-        def body(c, carry):
-            project(h, c)
-            return carry
-
-        lax.fori_loop(lo, hi, body, 0)
+        kv[h, lo:hi] = nn(lhs, rhs).astype(BF16).reshape(hi - lo, DSEQ, CROWS, 2 * GW)
 
     def attend_range(h, lo, hi):
         def body(t, carry):
@@ -393,68 +396,85 @@
     rows_copy.wait()
     fill()
     pl.semaphore_wait(barrier, len(peers))
-    for h in range(GROUPS):
-        w_begin(h)
-    for c in range(6):
-        rows_out(c)
+    rows_out(0)
+    rows_out(1)
+    rows_out(2)
+    rows_out(3)
+    rows_out(4)
+    rows_out(5)
+    w_begin(0)
+    w_begin(1)
     w_first(0)
     rows_out(6)
     rows_out(7)
     stage1(0)
+    stage1(1)
     stage2(0)
-    stage1(1)
+    stage1(2)
+    stage2(1)
     stage3(0)
-    stage2(1)
-    stage1(2)
-    stage3(1)
     stage1(3)
     stage2(2)
-    stage3(2)
+    rows_in(0)
+    stage3(1)
     stage1(4)
     stage2(3)
+    rows_in(1)
     stage1(5)
-    stage3(3)
+    stage3(2)
     stage2(4)
     w_step(0, 1)
-    stage3(4)
+    w_first(1)
+    stage3(3)
+    rows_in(2)
     stage2(5)
     stage1(6)
+    rows_in(3)
+    stage3(4)
+    stage1(7)
     stage3(5)
-    stage1(7)
+    rows_in(4)
+    w_step(0, 2)
     stage2(6)
+    stage2(7)
+    rows_in(5)
+    w_step(1, 1)
     stage3(6)
-    w_step(0, 2)
-    stage2(7)
-    w_first(1)
     stage3(7)
     w_step(0, 3)
-    w_step(1, 1)
+    rows_in(6)
+    rows_in(7)
+    w_step(1, 2)
     w_last(0)
-    for c in range(CHUNKS):
-        rows_in(c)
     w_in(0)
-    project_range(0, 0, CHUNKS)
-    w_step(1, 2)
+    project_range(0, 0, 4)
+    project_range(0, 4, 7)
+    project_range(0, 7, 8)
     for copy in late:
         copy.wait()
-    attend_range(0, 0, 8)
+    attend_range(0, 0, 2)
     w_step(1, 3)
+    attend_range(0, 2, 4)
+    attend_range(0, 4, 6)
+    attend_range(0, 6, 8)
     blocks(0)
     w_last(1)
     w_in(1)
     project_range(1, 0, 4)
+    project_range(1, 4, 8)
+    attend_range(1, 0, 2)
     chain3(0)
-    project_range(1, 4, 8)
+    attend_range(1, 2, 4)
+    attend_range(1, 4, 6)
+    attend_range(1, 6, 8)
+    blocks(1)
     chain2(0)
-    attend_range(1, 0, 4)
     partner(0)
+    chain3(1)
     chain1(0)
-    attend_range(1, 4, 8)
-    blocks(1)
-    chain0(0)
-    chain3(1)
     chain2(1)
     partner(1)
+    chain0(0)
     chain1(1)
     chain0(1)
     for copy in sent:
@@ -463,13 +483,18 @@
         drain(h)
 
 
+def hand_over(*refs):
+    for i in range(3):
+        refs[3 + i][...] = refs[i][...]
+
+
 def per_device(encoder_rows, w_key, w_value, query, grad_context, source):
     rows, inner = w_key.shape
     vmem = pl.BlockSpec(memory_space=pltpu.VMEM)
     hbm = pl.BlockSpec(memory_space=pl.ANY)
     dma = pltpu.SemaphoreType.DMA
     wide = 2 * GW
-    return pl.pallas_call(
+    outs = pl.pallas_call(
         kernel,
         out_shape=(
             jax.ShapeDtypeStruct(query.shape, BF16),
@@ -507,6 +532,13 @@
         ),
         name="cross_attention",
     )(source, encoder_rows, w_key, w_value, query, grad_context)
+    return pl.pallas_call(
+        hand_over,
+        out_shape=tuple(jax.ShapeDtypeStruct(o.shape, o.dtype) for o in outs),
+        in_specs=[vmem] * 3,
+        out_specs=(vmem,) * 3,
+        name="hand_over",
+    )(*outs)
 
 
 def solution(mesh):

time: 171 us -> 158 us (0.924)
  Pallas kernels: 164 us -> 157 us
  local copies, waits for them, and re-layouts: 5.6 us -> 0 us
    pallas_call x1, Pallas kernels: 164 us -> 155 us  [per_device(): pl.pallas_call(kernel, out_shape=(jax.ShapeDtypeStruct(query.shape, BF16)...]
    unnamed x3 -> x0, local copies, waits for them, and re-layouts: 5.6 us -> none
    pallas_call x0 -> x1, Pallas kernels: none -> 2.53 us  [per_device(): pl.pallas_call(hand_over, out_shape=tuple((jax.ShapeDtypeStruct(o.shape,...]
where the time goes in v5:
time: 158 us
  Pallas kernels  157 us (99%)
    pallas_call x1, Pallas kernels, per_device(): pl.pallas_call(kernel, out_shape=(jax.ShapeDtypeStruct(query.shape, BF16)...  155 us

profile of v5, /device:TPU:1, one launch (start us, length us, event | category | flops | bytes accessed | tf_op | source)
XLA Modules:
  0.0 157.8 jit_solution(6299102866220140902)
XLA Ops:
  0.6 154.7 %cross_attention.1 = (bf16[4,128,512]{2,1,0:T(8,128)(2,1)}, bf16[4,128,512]{2,1,0:T(8,128)(2,1)}, f32[2,128,512]{2,1,0:T(8,128)}) custom-call(s32[128]{0:T(128)} %src_ref.1, bf16[3,256,4096]{2,1,0:T(8,128)(2,1)} %e_hbm.1, bf16[128,512]{1,0:T(8,128)(2,1)} %wk_hbm.1, bf16[128,512]{1,0:T(8,128)(2,1)} %wv_hbm.1, bf16[4,128,512]{2,1,0:T(8,128)(2,1)} %q_hbm.1, ...), custom_call_target="tpu_custom_call" | custom-call | tf_op jit(solution)/shard_map/cross_attention/pallas_call | solution.py:497
  155.3 2.5 %hand_over.1 = (bf16[4,128,512]{2,1,0:T(8,128)(2,1)}, bf16[4,128,512]{2,1,0:T(8,128)(2,1)}, f32[2,128,512]{2,1,0:T(8,128)}) custom-call(bf16[4,128,512]{2,1,0:T(8,128)(2,1)} %get-tuple-element.6.refs_0_, bf16[4,128,512]{2,1,0:T(8,128)(2,1)} %get-tuple-element.7.refs_1_, f32[2,128,512]{2,1,0:T(8,128)} %get-tuple-element.8.refs_2_), custom_call_target="tpu_custom_call" | custom-call | tf_op jit(solution)/shard_map/hand_over/pallas_call | solution.py:535

commit v6 on v5

--- a/solution.py
+++ b/solution.py
@@ -22,9 +22,10 @@
 GROUPS = 2
 GW = SLICE // GROUPS
 PAIRS = GW // LANES
+ON_Z = (2, 3,)
 ORDER = (4, 3, 5, 2, 6, 1, 7)
 LIGHT = (7,)
-GATHER_COPIES = 15 * CHUNKS + 2 * len(LIGHT) + 17 * GROUPS
+GATHER_COPIES = 15 * CHUNKS + 2 * len(LIGHT) + 27 * GROUPS
 
 
 def nt(a, b):
@@ -173,6 +174,7 @@
     w_y, w_own = [None] * GROUPS, [None] * GROUPS
     wz = [{} for h in range(GROUPS)]
     from_sib = [[] for h in range(GROUPS)]
+    w_yrecv = [{} for h in range(GROUPS)]
 
     def wpair(h, k):
         return wf.at[h, core, (d + k + 8) % 8]
@@ -198,29 +200,41 @@
         wz[h][-1] = put(both, both, zl)
         from_sib[h].append(put(both, both, sib))
 
+    def w_next(h, j, blk, row, rows, to):
+        if j + 1 <= ON_Z[h]:
+            return put(blk, blk, to)
+        one = blk.at[row] if j < 3 or ON_Z[h] == 3 else blk.at[ylo, rows]
+        return put(one, one, to)
+
     def w_step(h, j):
+        half_rows = WROWS // 2
         wz[h][j].wait_recv()
         right = wpair(h, -j)
-        if j < 3:
-            wz[h][j + 1] = put(right, right, zr)
-        else:
-            one = right.at[ylo]
-            wz[h][4] = put(one, one, zr)
+        wz[h][j + 1] = w_next(h, j, right, ylo, pl.ds(0, half_rows), zr)
         wz[h][-j].wait_recv()
         left = wpair(h, j)
-        if j < 3:
-            wz[h][-j - 1] = put(left, left, zl)
-        else:
-            one = left.at[1 - ylo]
-            wz[h][-4] = put(one, one, zl)
-        from_sib[h].append(put(right, right, sib))
-        from_sib[h].append(put(left, left, sib))
+        row = 1 - ylo if j == 3 and ON_Z[h] == 3 else ylo
+        wz[h][-j - 1] = w_next(h, j, left, row, pl.ds(half_rows, half_rows), zl)
+        for k, blk in ((j, right), (-j, left)):
+            if j > ON_Z[h]:
+                one = blk.at[ylo]
+                w_yrecv[h][k] = put(one, one, ypart)
+                blk = one
+            from_sib[h].append(put(blk, blk, sib))
 
     def w_last(h):
         wz[h][4].wait_recv()
         wz[h][-4].wait_recv()
         far = wpair(h, 4)
+        if ON_Z[h] < 3:
+            far = far.at[ylo]
+            w_yrecv[h][4] = put(far, far, ypart)
         from_sib[h].append(put(far, far, sib))
+
+    def w_side(h, k):
+        w_yrecv[h][k].wait_recv()
+        blk = wpair(h, -k).at[1 - ylo]
+        from_sib[h].append(put(blk, blk, sib))
 
     def w_in(h):
         for copy in from_sib[h]:
@@ -400,13 +414,11 @@
     rows_out(1)
     rows_out(2)
     rows_out(3)
-    rows_out(4)
-    rows_out(5)
     w_begin(0)
     w_begin(1)
     w_first(0)
-    rows_out(6)
-    rows_out(7)
+    rows_out(4)
+    rows_out(5)
     stage1(0)
     stage1(1)
     stage2(0)
@@ -416,46 +428,51 @@
     stage1(3)
     stage2(2)
     rows_in(0)
+    w_step(0, 1)
+    rows_out(6)
+    rows_out(7)
     stage3(1)
-    stage1(4)
     stage2(3)
     rows_in(1)
+    stage1(4)
+    stage3(2)
+    stage3(3)
     stage1(5)
-    stage3(2)
     stage2(4)
-    w_step(0, 1)
+    rows_in(2)
+    w_step(0, 2)
     w_first(1)
-    stage3(3)
-    rows_in(2)
+    rows_in(3)
     stage2(5)
+    stage3(4)
     stage1(6)
-    rows_in(3)
-    stage3(4)
+    rows_in(4)
+    stage3(5)
     stage1(7)
-    stage3(5)
-    rows_in(4)
-    w_step(0, 2)
     stage2(6)
+    w_step(0, 3)
+    rows_in(5)
     stage2(7)
-    rows_in(5)
     w_step(1, 1)
+    w_side(0, 3)
+    w_last(0)
     stage3(6)
+    w_side(0, -3)
     stage3(7)
-    w_step(0, 3)
+    w_side(0, 4)
+    w_step(1, 2)
+    w_in(0)
+    rows_in(7)
+    project_range(0, 0, 4)
+    project_range(0, 7, 8)
     rows_in(6)
-    rows_in(7)
-    w_step(1, 2)
-    w_last(0)
-    w_in(0)
-    project_range(0, 0, 4)
     project_range(0, 4, 7)
-    project_range(0, 7, 8)
     for copy in late:
         copy.wait()
     attend_range(0, 0, 2)
-    w_step(1, 3)
     attend_range(0, 2, 4)
     attend_range(0, 4, 6)
+    w_step(1, 3)
     attend_range(0, 6, 8)
     blocks(0)
     w_last(1)

time: 158 us -> 155 us (0.981)
  Pallas kernels: 157 us -> 154 us
    pallas_call x1, Pallas kernels: 155 us -> 151 us  [per_device(): pl.pallas_call(kernel, out_shape=(jax.ShapeDtypeStruct(query.shape, BF16)...]
where the time goes in v6:
time: 155 us
  Pallas kernels  154 us (99%)
    pallas_call x1, Pallas kernels, per_device(): pl.pallas_call(kernel, out_shape=(jax.ShapeDtypeStruct(query.shape, BF16)...  151 us

profile of v6, /device:TPU:1, one launch (start us, length us, event | category | flops | bytes accessed | tf_op | source)
XLA Modules:
  0.0 154.5 jit_solution(8486799436910180054)
XLA Ops:
  0.6 151.3 %cross_attention.1 = (bf16[4,128,512]{2,1,0:T(8,128)(2,1)}, bf16[4,128,512]{2,1,0:T(8,128)(2,1)}, f32[2,128,512]{2,1,0:T(8,128)}) custom-call(s32[128]{0:T(128)} %src_ref.1, bf16[3,256,4096]{2,1,0:T(8,128)(2,1)} %e_hbm.1, bf16[128,512]{1,0:T(8,128)(2,1)} %wk_hbm.1, bf16[128,512]{1,0:T(8,128)(2,1)} %wv_hbm.1, bf16[4,128,512]{2,1,0:T(8,128)(2,1)} %q_hbm.1, ...), custom_call_target="tpu_custom_call" | custom-call | tf_op jit(solution)/shard_map/cross_attention/pallas_call | solution.py:514
  152.0 2.5 %hand_over.1 = (bf16[4,128,512]{2,1,0:T(8,128)(2,1)}, bf16[4,128,512]{2,1,0:T(8,128)(2,1)}, f32[2,128,512]{2,1,0:T(8,128)}) custom-call(bf16[4,128,512]{2,1,0:T(8,128)(2,1)} %get-tuple-element.6.refs_0_, bf16[4,128,512]{2,1,0:T(8,128)(2,1)} %get-tuple-element.7.refs_1_, f32[2,128,512]{2,1,0:T(8,128)} %get-tuple-element.8.refs_2_), custom_call_target="tpu_custom_call" | custom-call | tf_op jit(solution)/shard_map/hand_over/pallas_call | solution.py:552

commit v7 on v6

--- a/solution.py
+++ b/solution.py
@@ -284,12 +284,16 @@
 
     half = WROWS // 2
 
-    def to_z(h, k):
+    def to_z(h, k, r):
         to = zr if k % 2 == 0 else zl
-        if k < 2:
-            rows = pl.ds(k * half, half)
-            return remote(zsend.at[h, k, rows], zrecv.at[h, k, rows], z_s.at[h, k], z_r.at[h, k], to)
-        return remote(zsend.at[h, k], zrecv.at[h, k], z_s.at[h, k], z_r.at[h, k], to)
+        rows = pl.ds(r * half, half)
+        return remote(
+            zsend.at[h, k, rows], zrecv.at[h, k, rows], z_s.at[h, k, r], z_r.at[h, k, r], to
+        )
+
+    def z_rows(k, i):
+        r = (1, 0)[i] if k == 0 else i
+        return r, slice(r * half, (r + 1) * half), slice(WROWS + r * half, WROWS + (r + 1) * half)
 
     def columns(yy, cc, dd):
         block = (yy * 2 + cc) * 8 + dd
@@ -308,9 +312,9 @@
         to_y(h, 0).wait_recv()
         total = own[h, 0, WROWS:] + yrecv[h, 0].astype(F32)
         zsend[h, 0, :half] = total[:half].astype(BF16)
-        to_z(h, 0).start()
+        to_z(h, 0, 0).start()
         zsend[h, 1, half:] = total[half:].astype(BF16)
-        to_z(h, 1).start()
+        to_z(h, 1, 1).start()
 
     def blocks(h):
         def step(i, carry):
@@ -346,28 +350,33 @@
         absorb(h, 7)
 
     def chain3(h):
-        to_y(h, 1).wait_recv()
-        total = own[h, 1, WROWS:] + yrecv[h, 1].astype(F32)
-        to_z(h, 0).wait_recv()
-        zsend[h, 2, :half] = (total[:half] + zrecv[h, 0, :half].astype(F32)).astype(BF16)
-        zsend[h, 2, half:] = total[half:].astype(BF16)
-        to_z(h, 2).start()
-        to_y(h, 2).wait_recv()
-        total = own[h, 2, WROWS:] + yrecv[h, 2].astype(F32)
-        to_z(h, 1).wait_recv()
-        zsend[h, 3, :half] = total[:half].astype(BF16)
-        zsend[h, 3, half:] = (total[half:] + zrecv[h, 1, half:].astype(F32)).astype(BF16)
-        to_z(h, 3).start()
+        for k in range(2):
+            to_y(h, 1 + k).wait_recv()
+            for i in range(2):
+                r, rows, mine = z_rows(k, i)
+                part = own[h, 1 + k, mine] + yrecv[h, 1 + k, rows].astype(F32)
+                if r == k:
+                    to_z(h, k, k).wait_recv()
+                    part = part + zrecv[h, k, rows].astype(F32)
+                zsend[h, 2 + k, rows] = part.astype(BF16)
+                to_z(h, 2 + k, r).start()
         for k in range(2):
             to_p(h, k).wait_recv()
             psend[h, 2 + k] = (own[h, 5 + k, :WROWS] + precv[h, k].astype(F32)).astype(BF16)
             to_p(h, 2 + k).start()
 
+    def chain_step(h, j):
+        at = 2 * (3 - j)
+        for i in range(2):
+            for k in range(2):
+                r, rows, mine = z_rows(k, i)
+                to_z(h, at + k, r).wait_recv()
+                part = own[h, at + 1 + k, mine] + zrecv[h, at + k, rows].astype(F32)
+                zsend[h, at + 2 + k, rows] = part.astype(BF16)
+                to_z(h, at + 2 + k, r).start()
+
     def chain2(h):
-        for k in range(2):
-            to_z(h, 2 + k).wait_recv()
-            zsend[h, 4 + k] = (own[h, 3 + k, WROWS:] + zrecv[h, 2 + k].astype(F32)).astype(BF16)
-            to_z(h, 4 + k).start()
+        chain_step(h, 2)
 
     def partner(h):
         total = own[h, 7, :WROWS]
@@ -378,15 +387,13 @@
         to_y(h, 3).start()
 
     def chain1(h):
-        for k in range(2):
-            to_z(h, 4 + k).wait_recv()
-            zsend[h, 6 + k] = (own[h, 5 + k, WROWS:] + zrecv[h, 4 + k].astype(F32)).astype(BF16)
-            to_z(h, 6 + k).start()
+        chain_step(h, 1)
 
     def chain0(h):
         total = own[h, 7, WROWS:]
         for k in range(2):
-            to_z(h, 6 + k).wait_recv()
+            for r in range(2):
+                to_z(h, 6 + k, r).wait_recv()
             total = total + zrecv[h, 6 + k].astype(F32)
         to_y(h, 3).wait_recv()
         total = total + yrecv[h, 3].astype(F32)
@@ -397,7 +404,8 @@
     def drain(h):
         for k in range(8):
             to_sib(h, k).wait_send()
-            to_z(h, k).wait_send()
+            for r in (k,) if k < 2 else range(2):
+                to_z(h, k, r).wait_send()
         for k in range(4):
             to_y(h, k).wait_send()
             to_p(h, k).wait_send()
@@ -542,7 +550,7 @@
             pltpu.VMEM((GROUPS, 8, rows, wide), BF16),
             dma((GATHER_COPIES,)), dma((GATHER_COPIES,)), dma((3 + 2 * GROUPS + CHUNKS,)),
             dma((GROUPS, 8)), dma((GROUPS, 8)), dma((GROUPS, 4)), dma((GROUPS, 4)),
-            dma((GROUPS, 4)), dma((GROUPS, 4)), dma((GROUPS, 8)), dma((GROUPS, 8)),
+            dma((GROUPS, 4)), dma((GROUPS, 4)), dma((GROUPS, 8, 2)), dma((GROUPS, 8, 2)),
         ],
         compiler_params=pltpu.CompilerParams(
             collective_id=0, has_side_effects=True, vmem_limit_bytes=61 * 2**20

time: 155 us -> 154 us (level)
  no operation moved by 1% of the time
where the time goes in v7:
time: 154 us
  Pallas kernels  153 us (99%)
    pallas_call x1, Pallas kernels, per_device(): pl.pallas_call(kernel, out_shape=(jax.ShapeDtypeStruct(query.shape, BF16)...  151 us

profile of v7, /device:TPU:1, one launch (start us, length us, event | category | flops | bytes accessed | tf_op | source)
XLA Modules:
  0.0 154.1 jit_solution(16305256948557644953)
XLA Ops:
  0.6 150.9 %cross_attention.1 = (bf16[4,128,512]{2,1,0:T(8,128)(2,1)}, bf16[4,128,512]{2,1,0:T(8,128)(2,1)}, f32[2,128,512]{2,1,0:T(8,128)}) custom-call(s32[128]{0:T(128)} %src_ref.1, bf16[3,256,4096]{2,1,0:T(8,128)(2,1)} %e_hbm.1, bf16[128,512]{1,0:T(8,128)(2,1)} %wk_hbm.1, bf16[128,512]{1,0:T(8,128)(2,1)} %wv_hbm.1, bf16[4,128,512]{2,1,0:T(8,128)(2,1)} %q_hbm.1, ...), custom_call_target="tpu_custom_call" | custom-call | tf_op jit(solution)/shard_map/cross_attention/pallas_call | solution.py:522
  151.6 2.5 %hand_over.1 = (bf16[4,128,512]{2,1,0:T(8,128)(2,1)}, bf16[4,128,512]{2,1,0:T(8,128)(2,1)}, f32[2,128,512]{2,1,0:T(8,128)}) custom-call(bf16[4,128,512]{2,1,0:T(8,128)(2,1)} %get-tuple-element.6.refs_0_, bf16[4,128,512]{2,1,0:T(8,128)(2,1)} %get-tuple-element.7.refs_1_, f32[2,128,512]{2,1,0:T(8,128)} %get-tuple-element.8.refs_2_), custom_call_target="tpu_custom_call" | custom-call | tf_op jit(solution)/shard_map/hand_over/pallas_call | solution.py:560
